TPU v7x, 256 devices: a whole 4x4x8 slice. The times are simulated.
256 devices in a mesh: tm: 8 (over x, core), space: 32 (over y, z).
Axes of the slice: x: 4, y: 4, z: 8, core: 2. Of those that a mesh axis runs over, the one named last changes fastest.
Arguments:
- flux: float32 [8, 131072], P('tm', 'space'), may hold values from -6 to 6
- noise: float32 [8, 131072], P('tm', 'space'), may hold values from -6 to 6
- prior_scale: float32 [131072], P('space'), may hold values from 0.3 to 3
- footprints: bfloat16 [8, 1024, 32, 4096], P('tm', 'space'), may hold values from -0.09375 to 0.09375
- soundings: bfloat16 [8, 1024, 32], P('tm', 'space'), may hold values from -6 to 6
- targets: int32 [8, 1024, 1], P('tm', 'space'), may hold values from 0 to 31; in each aligned block of 32 rows (0 to 31, 32 to 63, ..., all dimensions but the last counted through in order) at most 2 rows name the same one
- basis: bfloat16 [131072, 256], P('space'), may hold values from -68 to 68
Outputs:
- proposal: float32 [8, 131072], P('tm', 'space')
- predicted: float32 [8, 1024, 32], P('tm', 'space')
- info_factor: float32 [256, 256], replicated
- whitened_rhs: float32 [256], replicated
Inputs may be any that keep to these rules, and one draw needn't show every extreme that they name: `targets`: in the rows of one device no tile is named more than 2 times, and in every draw some device names some tile exactly 2 times.
All inputs are finite; a program needn't handle non-finite values.
Results may differ from a plain program's by a relative error of at most 0.0047.
Values may be sent and summed in bfloat16 or wider, within the bound.
A program may use at most 128 MiB of HBM per device.

v0:
```python
import jax
import jax.numpy as jnp
from jax import lax
from jax.sharding import PartitionSpec as P

PATCH = 64
REACH = 8


BETA = 0.6
KEEP = 0.8


def padded(shard, sides, width):
    for axis, dim in sides:
        devices, length = (lax.axis_size(axis), shard.shape[dim])
        up = [(i, (i + 1) % devices) for i in range(devices - 1)]
        down = [(j, i) for i, j in up]
        last = lax.slice_in_dim(shard, length - width, length, axis=dim)
        leading = lax.slice_in_dim(shard, 0, width, axis=dim)
        before = lax.ppermute(last, axis, up)
        after = lax.ppermute(leading, axis, down)
        shard = jnp.concatenate([before, shard, after], axis=dim)
    return shard


def kernel_weights(reach):
    offsets = jnp.abs(jnp.arange(-reach, reach + 1).astype(jnp.float32))
    profile = (1.0 + 2.0 * offsets / reach) * jnp.exp(-2.0 * offsets / reach)
    return profile / jnp.sqrt(jnp.sum(profile * profile))


def finish_factor(gram_sum, projected):
    information = jnp.eye(gram_sum.shape[0], dtype=jnp.float32) + gram_sum
    factor_low = jnp.linalg.cholesky(information)
    rhs_value = jax.scipy.linalg.solve_triangular(factor_low, projected, lower=True)
    return (factor_low.T, rhs_value)


def per_device(flux, noise, prior_scale, footprints, soundings, targets, basis):
    tile_count = lax.axis_size("space")
    step_count = lax.axis_size("tm")
    block_count = footprints.shape[1]
    obs_count = footprints.shape[2]
    cell_count = footprints.shape[3]
    patch_edge = PATCH
    capacity = max(2, (2 * block_count + tile_count - 1) // tile_count)
    slot_count = tile_count * capacity
    weights = kernel_weights(REACH)
    extended = padded(noise, (("space", 1),), REACH * patch_edge)
    extended_grid = extended.reshape(patch_edge + 2 * REACH, patch_edge)
    row_offset = jnp.arange(patch_edge + 2 * REACH)[None, :] - jnp.arange(patch_edge)[:, None]
    col_offset = (
        jnp.arange(patch_edge)[:, None] - jnp.arange(patch_edge)[None, :] + REACH
    ) % patch_edge
    row_band = jnp.zeros((patch_edge, patch_edge + 2 * REACH), jnp.float32)
    col_circulant = jnp.zeros((patch_edge, patch_edge), jnp.float32)
    for position in range(2 * REACH + 1):
        row_band = row_band + weights[position] * (row_offset == position).astype(jnp.float32)
        col_circulant = col_circulant + weights[position] * (col_offset == position).astype(
            jnp.float32
        )
    along_rows = jnp.dot(row_band, extended_grid, precision=lax.Precision.HIGHEST)
    smooth = jnp.dot(along_rows, col_circulant, precision=lax.Precision.HIGHEST)
    proposal = KEEP * flux + BETA * prior_scale[None, :] * smooth.reshape(1, cell_count)
    destination = targets[0, :, 0]
    dest_onehot = (destination[:, None] == jnp.arange(tile_count)[None, :]).astype(jnp.int32)
    earlier = jnp.cumsum(dest_onehot, axis=0) - dest_onehot
    slot_rank = jnp.sum(earlier * dest_onehot, axis=1)
    slot_of = destination * capacity + slot_rank
    slot_match = slot_of[None, :] == jnp.arange(slot_count)[:, None]
    source_of = jnp.sum(jnp.where(slot_match, jnp.arange(block_count)[None, :] + 1, 0), axis=1) - 1
    source_of = jnp.where(source_of < 0, block_count, source_of)
    outgoing = jnp.take(footprints[0], source_of, axis=0, mode="fill", fill_value=0)
    sent_obs = jnp.take(soundings[0], source_of, axis=0, mode="fill", fill_value=0)
    outgoing = outgoing.reshape(tile_count, capacity, obs_count, cell_count)
    sent_obs = sent_obs.reshape(tile_count, capacity, obs_count)
    tile_half = proposal[0].astype(jnp.bfloat16)
    jac_scale = float(step_count * tile_count * block_count * obs_count) ** (-0.5)
    arrived, arrived_obs = (
        lax.all_to_all(outgoing, "space", split_axis=0, concat_axis=0, tiled=True),
        lax.all_to_all(sent_obs, "space", split_axis=0, concat_axis=0, tiled=True),
    )
    block_rows = arrived.reshape(slot_count * obs_count, cell_count)
    predicted_rows = jnp.dot(block_rows, tile_half, preferred_element_type=jnp.float32)
    jacobian = (jnp.dot(block_rows, basis, preferred_element_type=jnp.float32) * jac_scale).astype(
        jnp.bfloat16
    )
    misfit = arrived_obs.reshape(-1).astype(jnp.float32) - predicted_rows
    gram_sum = jnp.einsum("ra,rb->ab", jacobian, jacobian, preferred_element_type=jnp.float32)
    projected = jnp.dot(jacobian.astype(jnp.float32).T, misfit, precision=lax.Precision.HIGHEST)
    returned = lax.all_to_all(
        predicted_rows.reshape(tile_count, capacity, obs_count),
        "space",
        split_axis=0,
        concat_axis=0,
        tiled=True,
    )
    own_predicted = jnp.take(returned.reshape(slot_count, obs_count), slot_of, axis=0)
    tile_gram, tile_proj = lax.psum((gram_sum, projected), "space")
    window_gram, window_proj = lax.psum((tile_gram, tile_proj), "tm")
    factor_up, rhs_value = finish_factor(window_gram, window_proj)
    return (proposal, own_predicted[None], factor_up, rhs_value)


def solution(mesh):
    return jax.shard_map(
        per_device,
        mesh=mesh,
        in_specs=(
            P("tm", "space"),
            P("tm", "space"),
            P("space"),
            P("tm", "space", None, None),
            P("tm", "space", None),
            P("tm", "space", None),
            P("space", None),
        ),
        out_specs=(P("tm", "space"), P("tm", "space", None), P(), P()),
        check_vma=False,
    )
```

profile of v0, /device:TPU:1, one launch (start us, length us, event | category | flops | bytes accessed | tf_op | source)
XLA Modules:
  0.0 771.0 jit_solution(4540092611341958695)
XLA Ops:
  7.2 0.9 fusion.138
  8.1 0.8 select_reduce_fusion.3
  9.9 1.3 gather_fusion.2
  11.2 0.7 broadcast_select_fusion.1
  11.9 12.0 %all-to-all-start.2 = ((bf16[32,2,32]{2,1,0:T(2,128)(2,1)}), bf16[32,2,32]{2,1,0:T(2,128)(2,1)S(1)}, u32[]{:S(2)}, u32[]{:S(2)}) async-start(bf16[32,2,32]{2,1,0:T(2,128)(2,1)} %broadcast_select_fusion.1), calls=%async_computation.2 | async-start | bytes 32768 | tf_op jit(solution)/shard_map/all_to_all | solution.py:82
  23.9 10.8 %gather_fusion = bf16[64,32,4096]{2,1,0:T(8,128)(2,1)} fusion(bf16[32,32,4096]{2,1,0:T(8,128)(2,1)} %bitcast.111, s32[1024]{0:T(1024)S(1)} %pad_clamp_fusion.1), kind=kCustom, calls=%fused_computation | custom fusion | bytes 33554688 | tf_op jit(solution)/shard_map/jit(_take)/gather | solution.py:74
  34.7 14.0 %broadcast_select_fusion = bf16[32,2,32,4096]{3,2,1,0:T(8,128)(2,1)} fusion(bf16[32,2,32,4096]{3,2,1,0:T(8,128)(2,1)} %bitcast.110, pred[32,2]{1,0:T(8,128)(4,1)S(1)} %compare_and_fusion), kind=kLoop, calls=%fused_computation.5 | loop fusion | flops 8388608 | bytes 33554496 | tf_op jit(solution)/shard_map/jit(_take)/select_n | solution.py:74
  48.7 9.5 %all-to-all-start = ((bf16[32,2,32,4096]{3,2,1,0:T(8,128)(2,1)}), bf16[32,2,32,4096]{3,2,1,0:T(8,128)(2,1)}, u32[]{:S(2)}, u32[]{:S(2)}) async-start(bf16[32,2,32,4096]{3,2,1,0:T(8,128)(2,1)} %broadcast_select_fusion), calls=%async_computation | async-start | bytes 33554432 | tf_op jit(solution)/shard_map/all_to_all | solution.py:81
  58.3 3.1 collective-permute-start
  61.4 1.3 collective-permute-start.1
  64.8 348.7 %collective-permute-done = f32[1,512]{1,0:T(1,128)S(1)} collective-permute-done((f32[1,512]{1,0:T(1,128)S(1)}, f32[1,512]{1,0:T(1,128)S(1)}, u32[]{:S(2)}, u32[]{:S(2)}) %collective-permute-start) | collective-permute-done | bytes 2080 | tf_op jit(solution)/shard_map/ppermute | solution.py:21
  413.5 24.9 %collective-permute-done.1 = f32[1,512]{1,0:T(1,128)S(1)} collective-permute-done((f32[1,512]{1,0:T(1,128)S(1)}, f32[1,512]{1,0:T(1,128)S(1)}, u32[]{:S(2)}, u32[]{:S(2)}) %collective-permute-start.1) | collective-permute-done | bytes 2080 | tf_op jit(solution)/shard_map/ppermute | solution.py:22
  438.5 10.6 %fusion.47 = f32[64,64]{1,0:T(8,128)S(1)} fusion(f32[80,64]{1,0:T(8,128)S(1)} %reshape.174, f32[]{:T(128)} %bitcast.16, f32[]{:T(128)} %bitcast.15, f32[]{:T(128)} %bitcast.14, f32[]{:T(128)} %bitcast.13, f32[]{:T(128)} %bitcast.12, f32[]{:T(128)} %bitcast.11, f32[]{:T(128)} %bitcast.10, f32[]{:T(128)} %bitcast.9, f32[]{:T(128)} %bitcast.8, f32[]{:T(128)} %bitcast.7, ...), kind=kOutput, calls=%fused_computation.75 | convolution fusion | flops 4193280 | bytes 36932 | tf_op jit(solution)/shard_map/dot_general | solution.py:63
  449.1 10.6 %fusion.13 = f32[64,64]{1,0:T(8,128)S(1)} fusion(f32[64,64]{1,0:T(8,128)S(1)} %fusion.47, f32[]{:T(128)} %bitcast.16, f32[]{:T(128)} %bitcast.15, f32[]{:T(128)} %bitcast.14, f32[]{:T(128)} %bitcast.13, f32[]{:T(128)} %bitcast.12, f32[]{:T(128)} %bitcast.11, f32[]{:T(128)} %bitcast.10, f32[]{:T(128)} %bitcast.9, f32[]{:T(128)} %bitcast.8, f32[]{:T(128)} %bitcast.7, ...), kind=kOutput, calls=%fused_computation.41 | convolution fusion | flops 3403776 | bytes 32836 | tf_op jit(solution)/shard_map/dot_general | solution.py:64
  460.0 8.3 %fusion = bf16[2048,256]{1,0:T(8,128)(2,1)S(1)} fusion(bf16[2048,4096]{1,0:T(8,128)(2,1)} %bitcast.23, bf16[4096,256]{1,0:T(8,128)(2,1)S(1)} %copy-done), kind=kOutput, calls=%fused_computation.7 | convolution fusion | flops 4296015872 | bytes 19922944 | tf_op jit(solution)/shard_map/dot_general | solution.py:86
  468.3 1.2 fusion.256
  469.5 10.2 %fusion.135 = f32[1,2048]{1,0:T(1,128)S(1)} fusion(bf16[2048,4096]{1,0:T(8,128)(2,1)} %bitcast.23, f32[1,4096]{1,0:T(1,128)S(1)} %multiply_add_fusion), kind=kOutput, calls=%fused_computation.149 | convolution fusion | flops 16781312 | bytes 16801792 | tf_op jit(solution)/shard_map/dot_general | solution.py:85
  480.4 33.0 %all-to-all-start.1 = ((f32[32,2,32]{2,1,0:T(2,128)}), f32[32,2,32]{2,1,0:T(2,128)S(1)}, u32[]{:S(2)}, u32[]{:S(2)}) async-start(f32[32,2,32]{2,1,0:T(2,128)} %reshape.177), calls=%async_computation.1 | async-start | bytes 65536 | tf_op jit(solution)/shard_map/all_to_all | solution.py:92
  514.0 60.7 %psum.30 = f32[256]{0:T(256)S(1)} all-reduce(f32[256]{0:T(256)S(1)} %bitcast.121), channel_id=1, replica_groups=mesh['tm'=8,'space'=32] {'space'}, use_global_device_ids=true, to_apply=%region_10.11 | all-reduce | flops 256 | bytes 2048 | tf_op jit(solution)/shard_map/psum | solution.py:100
  574.6 27.2 %psum.31 = f32[256]{0:T(256)S(1)} all-reduce(f32[256]{0:T(256)S(1)} %psum.30), channel_id=1, replica_groups=mesh['tm'=8,'space'=32] {'tm'}, use_global_device_ids=true, to_apply=%region_11.12 | all-reduce | flops 256 | bytes 2048 | tf_op jit(solution)/shard_map/psum | solution.py:101
  602.4 31.3 %all-reduce.4.cloned.1.call-done = f32[256,256]{0,1:T(8,128)} async-done(((f32[256,256]{0,1:T(8,128)}), f32[256,256]{0,1:T(8,128)}) %all-reduce.4.cloned.1.call-update) | async-done | bytes 262160 | tf_op jit(solution)/shard_map/psum | solution.py:100
  634.4 65.9 %all-reduce.6.cloned.1.call-done = f32[256,256]{0,1:T(8,128)} async-done(((f32[256,256]{0,1:T(8,128)}), f32[256,256]{0,1:T(8,128)}) %all-reduce.6.cloned.1.call-update) | async-done | bytes 262160 | tf_op jit(solution)/shard_map/psum | solution.py:101
  700.2 1.0 convert_add_fusion
  701.4 1.0 fusion.5
  702.4 11.7 %cholesky.50 = f32[128,128]{1,0:T(8,128)S(1)} custom-call(f32[128,128]{1,0:T(8,128)S(1)} %cholesky.118), custom_call_target="Cholesky" | custom-call | tf_op jit(solution)/shard_map/jit(cholesky)/cholesky | solution.py:35
  714.1 9.8 %custom-call.15 = f32[1,128,128]{1,2,0:T(8,128)S(1)} custom-call(f32[1,128,128]{2,1,0:T(8,128)S(1)} %get-tuple-element.41), custom_call_target="InvertDiagBlocksLowerTriangular" | custom-call | tf_op jit(solution)/shard_map/jit(cholesky)/cholesky | solution.py:35
  724.4 11.7 %cholesky.105 = f32[128,128]{1,0:T(8,128)S(1)} custom-call(f32[128,128]{1,0:T(8,128)S(1)} %convolution_subtract_fusion), custom_call_target="Cholesky" | custom-call | tf_op jit(solution)/shard_map/jit(cholesky)/cholesky | solution.py:35
  738.2 4.0 while.1
  738.8 1.4 bitcast_dynamic-update-slice_fusion.2
  740.8 1.4 bitcast_dynamic-update-slice_fusion.2
  742.2 19.9 %custom-call.16 = f32[2,128,128]{1,2,0:T(8,128)S(1)} custom-call(f32[2,128,128]{2,1,0:T(8,128)S(1)} %get-tuple-element.11), custom_call_target="InvertDiagBlocksLowerTriangular" | custom-call | tf_op jit(solution)/shard_map/jit(_solve_triangular)/triangular_solve | solution.py:36
  763.3 0.8 copy.19
  (65 shorter events, 9.0 us)
Async XLA Ops:
  7.2 452.9 %copy-start = (bf16[4096,256]{1,0:T(8,128)(2,1)S(1)}, bf16[4096,256]{1,0:T(8,128)(2,1)}, u32[]{:S(2)}) copy-start(bf16[4096,256]{1,0:T(8,128)(2,1)} %param.13) | copy-start | bytes 6291460
  11.9 36.8 %all-to-all-start.2 = ((bf16[32,2,32]{2,1,0:T(2,128)(2,1)}), bf16[32,2,32]{2,1,0:T(2,128)(2,1)S(1)}, u32[]{:S(2)}, u32[]{:S(2)}) async-start(bf16[32,2,32]{2,1,0:T(2,128)(2,1)} %broadcast_select_fusion.1), calls=%async_computation.2 | async-start | bytes 32768 | tf_op jit(solution)/shard_map/all_to_all | solution.py:82
  48.7 9.6 %copy-start.2 = (f32[1,4096]{1,0:T(1,128)S(1)}, f32[1,4096]{1,0:T(1,128)}, u32[]{:S(2)}) copy-start(f32[1,4096]{1,0:T(1,128)} %param.8) | copy-start | bytes 49156
  48.7 15.3 %copy-start.5 = (s32[1,32,1]{1,2,0:T(1,128)S(1)}, s32[1,32,1]{1,2,0:T(1,128)}, u32[]{:S(2)}) copy-start(s32[1,32,1]{1,2,0:T(1,128)} %param.12) | copy-start | bytes 388
  48.7 411.1 %copy-start.3 = (f32[4096]{0:T(1024)S(1)}, f32[4096]{0:T(1024)}, u32[]{:S(2)}) copy-start(f32[4096]{0:T(1024)} %param.9) | copy-start | bytes 49156
  48.7 411.2 %copy-start.4 = (f32[1,4096]{1,0:T(1,128)S(1)}, f32[1,4096]{1,0:T(1,128)}, u32[]{:S(2)}) copy-start(f32[1,4096]{1,0:T(1,128)} %param.7) | copy-start | bytes 49156
  48.7 411.3 %all-to-all-start = ((bf16[32,2,32,4096]{3,2,1,0:T(8,128)(2,1)}), bf16[32,2,32,4096]{3,2,1,0:T(8,128)(2,1)}, u32[]{:S(2)}, u32[]{:S(2)}) async-start(bf16[32,2,32,4096]{3,2,1,0:T(8,128)(2,1)} %broadcast_select_fusion), calls=%async_computation | async-start | bytes 33554432 | tf_op jit(solution)/shard_map/all_to_all | solution.py:81
  58.3 575.4 %all-reduce.4.cloned.1.call-start = ((), (), s32[]{:S(2)}) async-start(), calls=%async_computation.3 | async-start | bytes 524288 | tf_op jit(solution)/shard_map/psum | solution.py:100
  58.3 355.1 %collective-permute-start = (f32[1,512]{1,0:T(1,128)S(1)}, f32[1,512]{1,0:T(1,128)S(1)}, u32[]{:S(2)}, u32[]{:S(2)}) collective-permute-start(f32[1,512]{1,0:T(1,128)S(1)} %get-tuple-element.42), channel_id=1, source_target_pairs={{0,1},{1,2},{2,3},{3,4},{4,5},{5,6},{6,7},{7,8},{8,9},{9,10},{10,1... | collective-permute-start | bytes 6152 | tf_op jit(solution)/shard_map/ppermute | solution.py:21
  61.4 377.0 %collective-permute-start.1 = (f32[1,512]{1,0:T(1,128)S(1)}, f32[1,512]{1,0:T(1,128)S(1)}, u32[]{:S(2)}, u32[]{:S(2)}) collective-permute-start(f32[1,512]{1,0:T(1,128)S(1)} %get-tuple-element.43), channel_id=1, source_target_pairs={{1,0},{2,1},{3,2},{4,3},{5,4},{6,5},{7,6},{8,7},{9,8},{10,9},{11,1... | collective-permute-start | bytes 6152 | tf_op jit(solution)/shard_map/ppermute | solution.py:22
  459.9 19.8 %copy-start.1 = (f32[1,4096]{1,0:T(1,128)}, f32[1,4096]{1,0:T(1,128)S(1)}, u32[]{:S(2)}) copy-start(f32[1,4096]{1,0:T(1,128)S(1)} %multiply_add_fusion) | copy-start | bytes 49156
  480.4 121.4 %all-to-all-start.1 = ((f32[32,2,32]{2,1,0:T(2,128)}), f32[32,2,32]{2,1,0:T(2,128)S(1)}, u32[]{:S(2)}, u32[]{:S(2)}) async-start(f32[32,2,32]{2,1,0:T(2,128)} %reshape.177), calls=%async_computation.1 | async-start | bytes 65536 | tf_op jit(solution)/shard_map/all_to_all | solution.py:92
  513.4 186.8 %all-reduce.6.cloned.1.call-start = ((), (), s32[]{:S(2)}) async-start(), calls=%async_computation.4 | async-start | bytes 524288 | tf_op jit(solution)/shard_map/psum | solution.py:101
Sparse Core Ops, SparseCore 0:
  469.7 163.9 all-reduce.3
  636.0 64.2 all-reduce.5
where the time goes:
time: 773 us; the launch traced here: 771 us
  waiting for transfers between devices  471 us (61%)
  blocking collectives  87.8 us (11%)
  other arithmetic  75.1 us (10%)
  starting transfers between devices  59 us (8%)
  matrix products  42.5 us (5%)
  local copies, waits for them, and re-layouts  19.4 us (3%)
  between operations  16.3 us (2%)
    ppermute x1, waiting for transfers between devices, padded(): before = lax.ppermute(last, axis, up)  349 us
    psum x1, waiting for transfers between devices, per_device(): window_gram, window_proj = lax.psum((tile_gram, tile_proj), 'tm')  65.9 us
    psum x1, blocking collectives, per_device(): tile_gram, tile_proj = lax.psum((gram_sum, projected), 'space')  60.7 us
    another operation x6, other arithmetic, finish_factor(): factor_low = jnp.linalg.cholesky(information)  34 us
    all_to_all x1, starting transfers between devices, per_device(): lax.all_to_all(predicted_rows.reshape(tile_count, capacity, obs_count), '...  33 us
    psum x1, waiting for transfers between devices, per_device(): tile_gram, tile_proj = lax.psum((gram_sum, projected), 'space')  31.3 us
    psum x1, blocking collectives, per_device(): window_gram, window_proj = lax.psum((tile_gram, tile_proj), 'tm')  27.2 us
    ppermute x1, waiting for transfers between devices, padded(): after = lax.ppermute(leading, axis, down)  24.9 us
  transfers between devices with their start and end apart: 7, of which 4 were waited for; matrix products, arithmetic and copies ran while one was open for 8% of the time, Pallas kernels for 0%

commit v1 on v0

v1 whole, which is shorter than its diff:
```python
import jax
import jax.numpy as jnp
from jax import lax
from jax.experimental import pallas as pl
from jax.experimental.pallas import tpu as pltpu
from jax.sharding import PartitionSpec as P

MESH = pl.DeviceIdType.MESH
BLOCKS_HERE = 32
JAC_SCALE = float(262144) ** (-0.5)

PATCH = 64
REACH = 8


BETA = 0.6
KEEP = 0.8


def padded(shard, sides, width):
    for axis, dim in sides:
        devices, length = (lax.axis_size(axis), shard.shape[dim])
        up = [(i, (i + 1) % devices) for i in range(devices - 1)]
        down = [(j, i) for i, j in up]
        last = lax.slice_in_dim(shard, length - width, length, axis=dim)
        leading = lax.slice_in_dim(shard, 0, width, axis=dim)
        before = lax.ppermute(last, axis, up)
        after = lax.ppermute(leading, axis, down)
        shard = jnp.concatenate([before, shard, after], axis=dim)
    return shard


def kernel_weights(reach):
    offsets = jnp.abs(jnp.arange(-reach, reach + 1).astype(jnp.float32))
    profile = (1.0 + 2.0 * offsets / reach) * jnp.exp(-2.0 * offsets / reach)
    return profile / jnp.sqrt(jnp.sum(profile * profile))


def finish_factor(gram_sum, projected):
    information = jnp.eye(gram_sum.shape[0], dtype=jnp.float32) + gram_sum
    factor_low = jnp.linalg.cholesky(information)
    rhs_value = jax.scipy.linalg.solve_triangular(factor_low, projected, lower=True)
    return (factor_low.T, rhs_value)


PA, PB, QA, QB = 368, 816, 560, 560
RX = 448
LAG1, LAG2 = 2, 4


def gather_kernel(tab_ref, mis_ref, fp_ref, basis_ref, aug_ref,
                  own_f, sib_f, tiles, jac, jac_out, tab_v, tab_own, tab_sib,
                  load_sem, pair_send, pair_recv, tree_recv, cross_recv, tree_send, cross_send,
                  jac_send, jac_recv):
    t = lax.axis_index("tm")
    s = lax.axis_index("space")
    x, c = lax.div(t, 2), lax.rem(t, 2)
    y, z = lax.div(s, 8), lax.rem(s, 8)
    sibling = (x * 2 + (1 - c), s)
    z_up = (t, y * 8 + lax.rem(z + 1, 8))
    z_down = (t, y * 8 + lax.rem(z + 7, 8))
    y_up = (t, lax.rem(y + 1, 4) * 8 + z)
    y_down = (t, lax.rem(y + 3, 4) * 8 + z)
    x_up = (lax.rem(x + 1, 4) * 2 + c, s)
    x_down = (lax.rem(x + 3, 4) * 2 + c, s)
    count = BLOCKS_HERE

    own_load = pltpu.make_async_copy(
        basis_ref.at[:, pl.ds(pl.multiple_of(c * 128, 128), 128)], tiles.at[s], load_sem.at[0])
    own_load.start()
    fp_load = pltpu.make_async_copy(fp_ref.at[0], own_f.at[pl.ds(0, count)], load_sem.at[1])
    fp_load.start()
    tab_load = pltpu.make_async_copy(tab_ref, tab_own, load_sem.at[2])
    tab_load.start()

    barrier = pltpu.get_barrier_semaphore()
    for other in (sibling, z_up, z_down, y_up, y_down, x_up, x_down):
        pl.semaphore_signal(barrier, inc=1, device_id=other, device_id_type=MESH)
    pl.semaphore_wait(barrier, 7)

    tab_swap = pltpu.make_async_remote_copy(
        src_ref=tab_ref, dst_ref=tab_v, send_sem=pair_send.at[0], recv_sem=pair_recv.at[0],
        device_id=sibling, device_id_type=MESH)
    tab_swap.start()
    own_load.wait()

    def send(rows, tile, send_sem, recv_sem, device):
        region = tiles.at[tile, rows]
        return pltpu.make_async_remote_copy(
            src_ref=region, dst_ref=region, send_sem=send_sem, recv_sem=recv_sem,
            device_id=device, device_id_type=MESH)

    classes = []
    start = 0
    for size, along_z_first, long_up in ((PA, True, True), (PB, True, False), (QA, False, True), (QB, False, False)):
        classes.append((pl.ds(start, size), along_z_first, long_up, False))
        start += size
    shared_base = start
    if RX:
        classes.append((pl.ds(pl.multiple_of(shared_base + x * RX, 16), RX), True, True, True))
    half = RX // 2

    def piece(owner, first, size):
        return pl.ds(pl.multiple_of(shared_base + owner * RX + first, 16), size)

    def tile_of(n):
        col, i = lax.div(n, 8), lax.rem(n, 8)
        dy = col + lax.div(col, 2) * (1 - 2 * lax.rem(col, 2))
        dz = lax.rem(lax.div(i + 1, 2) * (2 * lax.rem(i, 2) - 1) + 8, 8)
        tile = lax.rem(y - dy + 4, 4) * 8 + lax.rem(z - dz + 8, 8)
        return tile, dy, dz

    def forward(n):
        tile, dy, dz = tile_of(n)
        for k, (rows, along_z_first, long_up, shared) in enumerate(classes):
            hi_z, hi_y = (4, 2) if long_up else (3, 1)

            @pl.when(n > 0)
            def _():
                send(rows, tile, tree_send.at[k], tree_recv.at[k, tile], sibling).wait_recv()

            go_zu = jnp.logical_or(dz == 0, jnp.logical_and(dz >= 1, dz < hi_z))
            go_zd = jnp.logical_or(dz == 0, dz > hi_z + 1)
            go_yu = jnp.logical_or(dy == 0, jnp.logical_and(dy >= 1, dy < hi_y))
            go_yd = jnp.logical_or(dy == 0, dy > hi_y + 1)
            if along_z_first:
                go_zu, go_zd = jnp.logical_and(go_zu, dy == 0), jnp.logical_and(go_zd, dy == 0)
            else:
                go_yu, go_yd = jnp.logical_and(go_yu, dz == 0), jnp.logical_and(go_yd, dz == 0)
            for go, device in ((go_zu, z_up), (go_zd, z_down), (go_yu, y_up), (go_yd, y_down)):
                @pl.when(go)
                def _():
                    send(rows, tile, tree_send.at[k], tree_recv.at[k, tile], device).start()
            if shared:
                @pl.when(n > 0)
                def _():
                    send(rows, tile, cross_send.at[0], cross_recv.at[0, tile], x_up).start()
                    send(rows, tile, cross_send.at[1], cross_recv.at[1, tile], x_down).start()

    def pass_on(n):
        tile, _, _ = tile_of(n)
        below, above = lax.rem(x + 3, 4), lax.rem(x + 1, 4)
        send(piece(below, 0, RX), tile, cross_send.at[0], cross_recv.at[0, tile], sibling).wait_recv()
        send(piece(below, 0, half), tile, cross_send.at[2], cross_recv.at[2, tile], x_up).start()
        send(piece(above, 0, RX), tile, cross_send.at[1], cross_recv.at[1, tile], sibling).wait_recv()
        send(piece(above, half, half), tile, cross_send.at[3], cross_recv.at[3, tile], x_down).start()

    def multiply(n):
        tile, _, _ = tile_of(n)
        if RX:
            far = lax.rem(x + 2, 4)

            @pl.when(n > 0)
            def _():
                send(piece(far, 0, half), tile, cross_send.at[2], cross_recv.at[2, tile], sibling).wait_recv()
                send(piece(far, half, half), tile, cross_send.at[3], cross_recv.at[3, tile], sibling).wait_recv()
        own_a, own_b = tab_own[0, tile * 2], tab_own[0, tile * 2 + 1]
        sib_a, sib_b = tab_sib[0, tile * 2], tab_sib[0, tile * 2 + 1]
        total = jnp.zeros((128, 128), jnp.float32)
        for k in range(4096 // 512):
            ks = pl.ds(k * 512, 512)
            lhs = jnp.concatenate(
                [own_f[own_a, :, ks], own_f[own_b, :, ks], sib_f[sib_a, :, ks], sib_f[sib_b, :, ks]], axis=0)
            total += jnp.dot(lhs, tiles[tile, ks, :], preferred_element_type=jnp.float32)
        total = (total * JAC_SCALE).astype(jnp.bfloat16)
        rows = pl.ds(pl.multiple_of(tile * 64, 64), 64)
        jac[c, rows, :] = total[:64]
        jac_out[rows, :] = total[64:]
        pltpu.make_async_remote_copy(
            src_ref=jac_out.at[rows], dst_ref=jac.at[c, rows], send_sem=jac_send, recv_sem=jac_recv,
            device_id=sibling, device_id_type=MESH).start()

    forward(0)
    fp_swap = pltpu.make_async_remote_copy(
        src_ref=fp_ref.at[0], dst_ref=sib_f.at[pl.ds(0, count)], send_sem=pair_send.at[1],
        recv_sem=pair_recv.at[1], device_id=sibling, device_id_type=MESH)
    fp_swap.start()
    own_f[count] = jnp.zeros(own_f.shape[1:], own_f.dtype)
    sib_f[count] = jnp.zeros(sib_f.shape[1:], sib_f.dtype)
    tab_swap.wait()
    sib_load = pltpu.make_async_copy(tab_v, tab_sib, load_sem.at[3])
    sib_load.start()
    tab_load.wait()
    sib_load.wait()
    fp_load.wait()
    fp_swap.wait()

    def step(n, carry):
        @pl.when(n < 32)
        def _():
            forward(n)
        if RX:
            @pl.when(jnp.logical_and(n >= LAG1 + 1, n < 32 + LAG1))
            def _():
                pass_on(n - LAG1)
        lag = LAG2 if RX else 0

        @pl.when(n >= lag)
        def _():
            multiply(n - lag)
        return carry

    if RX:
        lax.fori_loop(1, 32 + LAG2, step, 0)
    else:
        multiply(jnp.int32(0))
        lax.fori_loop(1, 32, step, 0)

    for k, (rows, _, _, _) in enumerate(classes):
        region = tiles.at[pl.ds(0, 31), rows]
        pltpu.make_async_copy(region, region, tree_send.at[k]).wait()
    if RX:
        for k, size in enumerate((RX, RX, half, half)):
            region = tiles.at[pl.ds(0, 31), pl.ds(0, size)]
            pltpu.make_async_copy(region, region, cross_send.at[k]).wait()
    whole = pltpu.make_async_remote_copy(
        src_ref=jac_out, dst_ref=jac.at[1 - c], send_sem=jac_send, recv_sem=jac_recv,
        device_id=sibling, device_id_type=MESH)
    whole.wait()
    low, high = jac[0], jac[1]

    def gram(a, b):
        return lax.dot_general(a, b, (((0,), (0,)), ((), ())), preferred_element_type=jnp.float32)

    aug_ref[0:128, :] = gram(low, low)
    aug_ref[128:256, :] = gram(low, high)
    aug_ref[256:384, :] = gram(high, high)
    mis = mis_ref[...]
    mis_a = mis.astype(jnp.bfloat16)
    rest = mis - mis_a.astype(jnp.float32)
    mis_b = rest.astype(jnp.bfloat16)
    mis_c = (rest - mis_b.astype(jnp.float32)).astype(jnp.bfloat16)
    aug_ref[384:, :] = jnp.zeros((128, 128), jnp.float32)
    for k, side in enumerate((low, high)):
        part = sum(jnp.dot(m, side, preferred_element_type=jnp.float32) for m in (mis_c, mis_b, mis_a))
        aug_ref[384 + 8 * k:392 + 8 * k, :] = part


def gathered_information(table, misfit, footprints, basis):
    vm = pl.BlockSpec(memory_space=pltpu.VMEM)
    hbm = pl.BlockSpec(memory_space=pl.ANY)
    dma = pltpu.SemaphoreType.DMA
    return pl.pallas_call(
        gather_kernel,
        out_shape=jax.ShapeDtypeStruct((512, 128), jnp.float32),
        in_specs=[vm, vm, hbm, hbm],
        out_specs=vm,
        scratch_shapes=[
            pltpu.VMEM((33, 32, 4096), jnp.bfloat16),
            pltpu.VMEM((33, 32, 4096), jnp.bfloat16),
            pltpu.VMEM((32, 4096, 128), jnp.bfloat16),
            pltpu.VMEM((2, 2048, 128), jnp.bfloat16),
            pltpu.VMEM((2048, 128), jnp.bfloat16),
            pltpu.VMEM((1, 128), jnp.int32),
            pltpu.SMEM((1, 128), jnp.int32),
            pltpu.SMEM((1, 128), jnp.int32),
            dma((4,)), dma((2,)), dma((2,)), dma((5, 32)), dma((4, 32)), dma((5,)), dma((4,)),
            dma, dma,
        ],
        compiler_params=pltpu.CompilerParams(
            collective_id=0, has_side_effects=True, vmem_limit_bytes=60 * 1024 * 1024),
        name="gather_information",
    )(table, misfit, footprints, basis)


def per_device(flux, noise, prior_scale, footprints, soundings, targets, basis):
    block_count = footprints.shape[1]
    obs_count = footprints.shape[2]
    cell_count = footprints.shape[3]
    patch_edge = PATCH
    tile_count = 32
    weights = kernel_weights(REACH)
    extended = padded(noise, (("space", 1),), REACH * patch_edge)
    extended_grid = extended.reshape(patch_edge + 2 * REACH, patch_edge)
    row_offset = jnp.arange(patch_edge + 2 * REACH)[None, :] - jnp.arange(patch_edge)[:, None]
    col_offset = (
        jnp.arange(patch_edge)[:, None] - jnp.arange(patch_edge)[None, :] + REACH
    ) % patch_edge
    row_band = jnp.zeros((patch_edge, patch_edge + 2 * REACH), jnp.float32)
    col_circulant = jnp.zeros((patch_edge, patch_edge), jnp.float32)
    for position in range(2 * REACH + 1):
        row_band = row_band + weights[position] * (row_offset == position).astype(jnp.float32)
        col_circulant = col_circulant + weights[position] * (col_offset == position).astype(
            jnp.float32
        )
    along_rows = jnp.dot(row_band, extended_grid, precision=lax.Precision.HIGHEST)
    smooth = jnp.dot(along_rows, col_circulant, precision=lax.Precision.HIGHEST)
    proposal = KEEP * flux + BETA * prior_scale[None, :] * smooth.reshape(1, cell_count)
    destination = targets[0, :, 0]
    dest_onehot = destination[:, None] == jnp.arange(tile_count)[None, :]
    counts = dest_onehot.astype(jnp.int32)
    slot_rank = jnp.sum((jnp.cumsum(counts, axis=0) - counts) * counts, axis=1)
    slot_of = destination * 2 + slot_rank
    slot_match = slot_of[None, :] == jnp.arange(2 * tile_count)[:, None]
    source_of = jnp.sum(jnp.where(slot_match, jnp.arange(block_count)[None, :] + 1, 0), axis=1) - 1
    source_of = jnp.where(source_of < 0, block_count, source_of)
    table = jnp.zeros((1, 128), jnp.int32).at[0, : 2 * tile_count].set(source_of)
    all_half = lax.all_gather(proposal[0].astype(jnp.bfloat16), "space")
    every = jnp.dot(
        footprints[0].reshape(block_count * obs_count, cell_count), all_half.T,
        preferred_element_type=jnp.float32,
    ).reshape(block_count, obs_count, tile_count)
    predicted = jnp.sum(jnp.where(dest_onehot[:, None, :], every, 0.0), axis=2)
    misfit = soundings[0].astype(jnp.float32) - predicted
    misfit_slots = jnp.sum(jnp.where(slot_match[:, :, None], misfit[None], 0.0), axis=1)
    misfit_rows = jnp.zeros((8, 2048), jnp.float32).at[0].set(misfit_slots.reshape(-1))
    aug = gathered_information(table, misfit_rows, footprints, basis)
    aug = lax.psum(aug, ("tm", "space"))
    cross = aug[128:256]
    gram = jnp.block([[aug[0:128], cross], [cross.T, aug[256:384]]])
    projected = jnp.concatenate([aug[384], aug[392]])
    factor_up, rhs_value = finish_factor(gram, projected)
    return (proposal, predicted[None], factor_up, rhs_value)


def solution(mesh):
    return jax.shard_map(
        per_device,
        mesh=mesh,
        in_specs=(
            P("tm", "space"),
            P("tm", "space"),
            P("space"),
            P("tm", "space", None, None),
            P("tm", "space", None),
            P("tm", "space", None),
            P("space", None),
        ),
        out_specs=(P("tm", "space"), P("tm", "space", None), P(), P()),
        check_vma=False,
    )
```

time: 773 us -> 592 us (0.77)
  waiting for transfers between devices: 471 us -> 246 us
  Pallas kernels: 0 us -> 177 us
  starting transfers between devices: 59 us -> 5.69 us
  blocking collectives: 87.8 us -> 41.8 us
  matrix products: 42.5 us -> 28.9 us
  other arithmetic: 75.1 us -> 62 us
    ppermute x1, waiting for transfers between devices: 349 us -> 0.01 us  [padded(): before = lax.ppermute(last, axis, up)]
    pallas_call x0 -> x1, Pallas kernels: none -> 177 us  [gathered_information(): pl.pallas_call(gather_kernel, out_shape=jax.ShapeDtypeStruct((512, 128),...]
    psum x2 -> x1, waiting for transfers between devices: 97.2 us -> 246 us  [per_device(): aug = lax.psum(aug, ('tm', 'space'))]
    psum x2 -> x0, blocking collectives: 87.8 us -> none  [the longest x1 60.7 us: per_device(): tile_gram, tile_proj = lax.psum((gram_sum, projected), 'space')]
    all_to_all x3 -> x0, starting transfers between devices: 54.5 us -> none  [the longest x1 33 us: per_device(): lax.all_to_all(predicted_rows.reshape(tile_count, capacity, obs_count), '...]
    all_gather x0 -> x1, blocking collectives: none -> 41.8 us  [per_device(): all_half = lax.all_gather(proposal[0].astype(jnp.bfloat16), 'space')]
    ppermute x1, waiting for transfers between devices: 24.9 us -> 0.01 us  [padded(): after = lax.ppermute(leading, axis, down)]
    select_n x5 -> x0, other arithmetic: 15.4 us -> none  [the longest x2 14 us: per_device(): jnp.take(footprints[0], source_of, axis=0, mode='fill', fill_value=0)]
  transfers between devices with their start and end apart: 7 -> 3, of which waited for: 4 -> 1; matrix products, arithmetic and copies ran while one was open for 8% -> 1% of each run, Pallas kernels for 0% -> 0%
where the time goes in v1:
time: 592 us; the launch traced here: 590 us
  waiting for transfers between devices  246 us (42%)
  Pallas kernels  177 us (30%)
  other arithmetic  62 us (10%)
  blocking collectives  41.8 us (7%)
  matrix products  28.9 us (5%)
  between operations  16.3 us (3%)
  local copies, waits for them, and re-layouts  12.5 us (2%)
    psum x1, waiting for transfers between devices, per_device(): aug = lax.psum(aug, ('tm', 'space'))  246 us
    pallas_call x1, Pallas kernels, gathered_information(): pl.pallas_call(gather_kernel, out_shape=jax.ShapeDtypeStruct((512, 128),...  177 us
    all_gather x1, blocking collectives, per_device(): all_half = lax.all_gather(proposal[0].astype(jnp.bfloat16), 'space')  41.8 us
    another operation x6, other arithmetic, finish_factor(): factor_low = jnp.linalg.cholesky(information)  33.9 us
    another operation x4, other arithmetic, finish_factor(): jax.scipy.linalg.solve_triangular(factor_low, projected, lower=True)  20.5 us
  transfers between devices with their start and end apart: 3, of which 1 were waited for; matrix products, arithmetic and copies ran while one was open for 1% of the time, Pallas kernels for 0%

profile of v1, /device:TPU:1, one launch (start us, length us, event | category | flops | bytes accessed | tf_op | source)
XLA Modules:
  0.0 590.0 jit_solution(11803988696446989919)
XLA Ops:
  7.2 0.7 fusion.250
  7.9 4.4 collective-permute-start
  12.3 1.3 collective-permute-start.1
  13.6 0.6 multiply_reduce_fusion
  14.2 0.6 compare_reduce_fusion.2
  15.6 0.7 fusion.208
  16.3 0.8 select_reduce_fusion.4
  17.2 0.7 multiply_add_fusion.1
  18.0 0.7 broadcast_select_fusion
  18.7 0.7 fusion.251
  20.6 0.8 maximum_reduce_fusion
  21.4 10.9 %fusion.48 = f32[64,64]{1,0:T(8,128)S(1)} fusion(f32[80,64]{1,0:T(8,128)S(1)} %reshape.179, f32[]{:T(128)} %bitcast.16, f32[]{:T(128)} %bitcast.15, f32[]{:T(128)} %bitcast.14, f32[]{:T(128)} %bitcast.13, f32[]{:T(128)} %bitcast.12, f32[]{:T(128)} %bitcast.11, f32[]{:T(128)} %bitcast.10, f32[]{:T(128)} %bitcast.9, f32[]{:T(128)} %bitcast.8, f32[]{:T(128)} %bitcast.7, ...), kind=kOutput, calls=%fused_computation.73 | convolution fusion | flops 4193280 | bytes 36932 | tf_op jit(solution)/shard_map/dot_general | solution.py:286
  32.3 10.9 %fusion.14 = f32[64,64]{1,0:T(8,128)S(1)} fusion(f32[64,64]{1,0:T(8,128)S(1)} %fusion.48, f32[]{:T(128)} %bitcast.16, f32[]{:T(128)} %bitcast.15, f32[]{:T(128)} %bitcast.14, f32[]{:T(128)} %bitcast.13, f32[]{:T(128)} %bitcast.12, f32[]{:T(128)} %bitcast.11, f32[]{:T(128)} %bitcast.10, f32[]{:T(128)} %bitcast.9, f32[]{:T(128)} %bitcast.8, f32[]{:T(128)} %bitcast.7, ...), kind=kOutput, calls=%fused_computation.39 | convolution fusion | flops 3403776 | bytes 32836 | tf_op jit(solution)/shard_map/dot_general | solution.py:287
  43.3 0.7 multiply_multiply_fusion
  44.0 1.4 convert_bitcast_fusion
  45.4 41.8 %all-gather = bf16[32,1,4096]{2,1,0:T(2,128)(2,1)S(1)} all-gather(bf16[1,1,4096]{2,1,0:T(2,128)(2,1)S(1)} %get-tuple-element.62), channel_id=1, replica_groups=mesh['tm'=8,'space'=32] {'space'}, dimensions={0}, use_global_device_ids=true | all-gather | bytes 270336 | tf_op jit(solution)/shard_map/all_gather | solution.py:298
  87.2 6.0 %fusion.1 = f32[1024]{0:T(1024)S(1)} fusion(pred[1024,32]{0,1:T(32,128)(4,1)S(1)} %broadcast_in_dim.74, bf16[1024,4096]{1,0:T(8,128)(2,1)} %bitcast.95, bf16[32,1,4096]{2,1,0:T(2,128)(2,1)S(1)} %all-gather), kind=kOutput, calls=%fused_computation.4 | convolution fusion | flops 268499968 | bytes 8687616 | tf_op jit(solution)/shard_map/dot_general | solution.py:299
  93.7 0.6 scatter.9.mis_ref
  94.3 176.6 %gather_information.1 = f32[512,128]{1,0:T(8,128)} custom-call(s32[1,128]{1,0:T(1,128)} %scatter.6.tab_ref, f32[8,2048]{1,0:T(8,128)} %scatter.9.mis_ref, bf16[1,32,32,4096]{3,2,1,0:T(8,128)(2,1)} %fp_ref.1, bf16[4096,256]{1,0:T(8,128)(2,1)} %basis_ref.1), custom_call_target="tpu_custom_call" | custom-call | tf_op jit(solution)/shard_map/gather_information/pallas_call | solution.py:243
  271.0 1.8 copy.28
  272.8 246.3 %all-reduce.5.cloned.1.call-done = f32[512,128]{0,1:T(8,128)} async-done(((f32[512,128]{0,1:T(8,128)}), f32[512,128]{0,1:T(8,128)}) %all-reduce.5.cloned.1.call-update) | async-done | bytes 262160 | tf_op jit(solution)/shard_map/psum | solution.py:308
  519.0 0.9 fusion.249
  520.3 11.7 %cholesky.50 = f32[128,128]{1,0:T(8,128)S(1)} custom-call(f32[128,128]{1,0:T(8,128)S(1)} %cholesky.118), custom_call_target="Cholesky" | custom-call | tf_op jit(solution)/shard_map/jit(cholesky)/cholesky | solution.py:41
  532.1 9.8 %custom-call.15 = f32[1,128,128]{1,2,0:T(8,128)S(1)} custom-call(f32[1,128,128]{2,1,0:T(8,128)S(1)} %get-tuple-element.75), custom_call_target="InvertDiagBlocksLowerTriangular" | custom-call | tf_op jit(solution)/shard_map/jit(cholesky)/cholesky | solution.py:41
  542.4 11.7 %cholesky.105 = f32[128,128]{1,0:T(8,128)S(1)} custom-call(f32[128,128]{1,0:T(8,128)S(1)} %convolution_subtract_fusion), custom_call_target="Cholesky" | custom-call | tf_op jit(solution)/shard_map/jit(cholesky)/cholesky | solution.py:41
  554.1 0.6 compare_reduce_fusion
  556.3 0.8 copy.31
  557.2 4.0 while.3
  557.8 1.4 bitcast_dynamic-update-slice_fusion.2
  559.8 1.4 bitcast_dynamic-update-slice_fusion.2
  561.2 19.7 %custom-call.16 = f32[2,128,128]{1,2,0:T(8,128)S(1)} custom-call(f32[2,128,128]{2,1,0:T(8,128)S(1)} %get-tuple-element.35), custom_call_target="InvertDiagBlocksLowerTriangular" | custom-call | tf_op jit(solution)/shard_map/jit(_solve_triangular)/triangular_solve | solution.py:42
  580.9 1.1 slice_reduce_fusion.1
  (46 shorter events, 5.5 us)
Async XLA Ops:
  7.2 86.1 %copy-start.1 = (bf16[1,32,32]{2,1,0:T(8,128)(2,1)S(1)}, bf16[1,32,32]{2,1,0:T(8,128)(2,1)}, u32[]{:S(2)}) copy-start(bf16[1,32,32]{2,1,0:T(8,128)(2,1)} %param.15) | copy-start | bytes 6148
  7.2 511.9 %all-reduce.5.cloned.1.call-start = ((), (), s32[]{:S(2)}) async-start(), calls=%async_computation | async-start | bytes 524288 | tf_op jit(solution)/shard_map/psum | solution.py:308
  7.9 12.6 %collective-permute-start = (f32[1,512]{1,0:T(1,128)S(1)}, f32[1,512]{1,0:T(1,128)S(1)}, u32[]{:S(2)}, u32[]{:S(2)}) collective-permute-start(f32[1,512]{1,0:T(1,128)S(1)} %get-tuple-element.76), channel_id=1, source_target_pairs={{0,1},{1,2},{2,3},{3,4},{4,5},{5,6},{6,7},{7,8},{8,9},{9,10},{10,1... | collective-permute-start | bytes 6152 | tf_op jit(solution)/shard_map/ppermute | solution.py:27
  12.3 8.3 %collective-permute-start.1 = (f32[1,512]{1,0:T(1,128)S(1)}, f32[1,512]{1,0:T(1,128)S(1)}, u32[]{:S(2)}, u32[]{:S(2)}) collective-permute-start(f32[1,512]{1,0:T(1,128)S(1)} %get-tuple-element.77), channel_id=1, source_target_pairs={{1,0},{2,1},{3,2},{4,3},{5,4},{6,5},{7,6},{8,7},{9,8},{10,9},{11,1... | collective-permute-start | bytes 6152 | tf_op jit(solution)/shard_map/ppermute | solution.py:28
  93.3 463.9 %copy-start = (f32[1,32,32]{2,1,0:T(8,128)}, f32[1,32,32]{2,1,0:T(8,128)S(1)}, u32[]{:S(2)}) copy-start(f32[1,32,32]{2,1,0:T(8,128)S(1)} %broadcast_in_dim.76) | copy-start | bytes 12292
Sparse Core Ops, SparseCore 0:
  272.9 246.1 all-reduce.4

commit v2 on v1

--- a/solution.py
+++ b/solution.py
@@ -6,6 +6,7 @@
 from jax.sharding import PartitionSpec as P
 
 MESH = pl.DeviceIdType.MESH
+HIGHEST = lax.Precision.HIGHEST
 BLOCKS_HERE = 32
 JAC_SCALE = float(262144) ** (-0.5)
 
@@ -34,13 +35,6 @@
     offsets = jnp.abs(jnp.arange(-reach, reach + 1).astype(jnp.float32))
     profile = (1.0 + 2.0 * offsets / reach) * jnp.exp(-2.0 * offsets / reach)
     return profile / jnp.sqrt(jnp.sum(profile * profile))
-
-
-def finish_factor(gram_sum, projected):
-    information = jnp.eye(gram_sum.shape[0], dtype=jnp.float32) + gram_sum
-    factor_low = jnp.linalg.cholesky(information)
-    rhs_value = jax.scipy.linalg.solve_triangular(factor_low, projected, lower=True)
-    return (factor_low.T, rhs_value)
 
 
 PA, PB, QA, QB = 368, 816, 560, 560
@@ -261,6 +255,146 @@
             collective_id=0, has_side_effects=True, vmem_limit_bytes=60 * 1024 * 1024),
         name="gather_information",
     )(table, misfit, footprints, basis)
+
+
+def factor_rows(work, out_u, out_v):
+    row = lax.broadcasted_iota(jnp.int32, (32, 128), 0)
+    lane = lax.broadcasted_iota(jnp.int32, (32, 128), 1)
+    wide_row = lax.broadcasted_iota(jnp.int32, (32, 256), 0)
+    wide_lane = lax.broadcasted_iota(jnp.int32, (32, 256), 1)
+    for k in range(8):
+        k0, c0 = 32 * k, 128 * (k // 4)
+        off = k0 - c0
+        eye0 = (off + 64) % 128
+        rows = work[k0:k0 + 32, :]
+        e = jnp.where(jnp.logical_and(lane >= off, lane < off + 32), rows[:, c0:c0 + 128], 0.0)
+        e = e + (lane - eye0 == row).astype(jnp.float32)
+        for j in range(32):
+            column = jnp.where(row > j, jnp.broadcast_to(e[:, off + j:off + j + 1], (32, 128)), 0.0)
+            pivot = e[j:j + 1, off + j:off + j + 1]
+            e = e - column * (e[j:j + 1, :] * (1.0 / pivot))
+        diagonal = jnp.sum(jnp.where(lane == row + off, e, 0.0), axis=1, keepdims=True)
+        e = e * lax.rsqrt(diagonal)
+        inverse = e[:, eye0:eye0 + 32]
+        panel = jnp.dot(inverse, rows[:, c0:], preferred_element_type=jnp.float32, precision=HIGHEST)
+        upper = panel[:, :256 - c0]
+        if c0:
+            upper = jnp.concatenate([jnp.zeros((32, c0), jnp.float32), upper], axis=1)
+        upper = jnp.where(wide_lane >= wide_row + k0, upper, 0.0)
+        out_u[k0:k0 + 32, :] = upper
+        out_v[k0:k0 + 32, :] = panel[:, 256 - c0:]
+        if k < 7:
+            k1 = k0 + 32
+            c1 = 128 * (k1 // 128)
+            left = panel[:, c1 - c0:256 - c0]
+            update = lax.dot_general(left, panel[:, c1 - c0:], (((0,), (0,)), ((), ())),
+                                     preferred_element_type=jnp.float32, precision=HIGHEST)
+            work[k1:, c1:] = work[k1:, c1:] - update[k1 - c1:]
+
+
+def finish_kernel(aug_ref, u_ref, v_ref, parts, sums, full, work,
+                  send_a, recv_a, send_b, recv_b, send_c, recv_c):
+    t = lax.axis_index("tm")
+    s = lax.axis_index("space")
+    x, c = lax.div(t, 2), lax.rem(t, 2)
+    y, z = lax.div(s, 8), lax.rem(s, 8)
+    a = c * 8 + z
+    b = x * 4 + y
+
+    def in_a(k):
+        other = lax.rem(a + k, 16)
+        return other, (x * 2 + lax.div(other, 8), y * 8 + lax.rem(other, 8))
+
+    def in_b(k):
+        other = lax.rem(b + k, 16)
+        return other, (lax.div(other, 4) * 2 + c, lax.rem(other, 4) * 8 + z)
+
+    barrier = pltpu.get_barrier_semaphore()
+
+    def greet(k, carry):
+        for group in (in_a, in_b):
+            pl.semaphore_signal(barrier, inc=1, device_id=group(k)[1], device_id_type=MESH)
+        return carry
+
+    lax.fori_loop(1, 16, greet, 0)
+    pl.semaphore_wait(barrier, 30)
+
+    def rows(index):
+        return pl.ds(pl.multiple_of(index * 32, 32), 32)
+
+    def scatter(k, carry):
+        other, device = in_a(k)
+        pltpu.make_async_remote_copy(
+            src_ref=aug_ref.at[rows(other)], dst_ref=parts.at[k - 1], send_sem=send_a, recv_sem=recv_a,
+            device_id=device, device_id_type=MESH).start()
+        return carry
+
+    lax.fori_loop(1, 16, scatter, 0)
+
+    def settle(region, send_sem, recv_sem):
+        pltpu.make_async_copy(region, region, send_sem).wait()
+        pltpu.make_async_copy(region, region, recv_sem).wait()
+
+    settle(parts, send_a, recv_a)
+    own = aug_ref[rows(a), :]
+    for k in range(15):
+        own = own + parts[k]
+    sums[b] = own
+
+    def exchange(k, carry):
+        _, device = in_b(k)
+        pltpu.make_async_remote_copy(
+            src_ref=sums.at[b], dst_ref=sums.at[b], send_sem=send_b, recv_sem=recv_b,
+            device_id=device, device_id_type=MESH).start()
+        return carry
+
+    lax.fori_loop(1, 16, exchange, 0)
+    settle(parts, send_b, recv_b)
+    total = sums[0]
+    for k in range(1, 16):
+        total = total + sums[k]
+    full[rows(a), :] = total
+
+    def spread(k, carry):
+        _, device = in_a(k)
+        pltpu.make_async_remote_copy(
+            src_ref=full.at[rows(a)], dst_ref=full.at[rows(a)], send_sem=send_c, recv_sem=recv_c,
+            device_id=device, device_id_type=MESH).start()
+        return carry
+
+    lax.fori_loop(1, 16, spread, 0)
+    settle(parts, send_c, recv_c)
+    square = (128, 128)
+    eye = (lax.broadcasted_iota(jnp.int32, square, 0) == lax.broadcasted_iota(jnp.int32, square, 1))
+    eye = eye.astype(jnp.float32)
+    rhs = full[384:512, :].T
+    work[0:128, 0:128] = full[0:128, :] + eye
+    work[0:128, 128:256] = full[128:256, :]
+    work[128:256, 128:256] = full[256:384, :] + eye
+    work[0:128, 256:384] = rhs
+    work[128:256, 256:384] = jnp.concatenate([rhs[:, 8:], rhs[:, :8]], axis=1)
+    factor_rows(work, u_ref, v_ref)
+
+
+def finished(aug):
+    vm = pl.BlockSpec(memory_space=pltpu.VMEM)
+    dma = pltpu.SemaphoreType.DMA
+    upper, rhs = pl.pallas_call(
+        finish_kernel,
+        out_shape=(jax.ShapeDtypeStruct((256, 256), jnp.float32), jax.ShapeDtypeStruct((256, 128), jnp.float32)),
+        in_specs=[vm],
+        out_specs=(vm, vm),
+        scratch_shapes=[
+            pltpu.VMEM((15, 32, 128), jnp.float32),
+            pltpu.VMEM((16, 32, 128), jnp.float32),
+            pltpu.VMEM((512, 128), jnp.float32),
+            pltpu.VMEM((256, 384), jnp.float32),
+            dma, dma, dma, dma, dma, dma,
+        ],
+        compiler_params=pltpu.CompilerParams(collective_id=1, has_side_effects=True),
+        name="sum_and_factor",
+    )(aug)
+    return upper, rhs[:, 0]
 
 
 def per_device(flux, noise, prior_scale, footprints, soundings, targets, basis):
@@ -305,11 +439,7 @@
     misfit_slots = jnp.sum(jnp.where(slot_match[:, :, None], misfit[None], 0.0), axis=1)
     misfit_rows = jnp.zeros((8, 2048), jnp.float32).at[0].set(misfit_slots.reshape(-1))
     aug = gathered_information(table, misfit_rows, footprints, basis)
-    aug = lax.psum(aug, ("tm", "space"))
-    cross = aug[128:256]
-    gram = jnp.block([[aug[0:128], cross], [cross.T, aug[256:384]]])
-    projected = jnp.concatenate([aug[384], aug[392]])
-    factor_up, rhs_value = finish_factor(gram, projected)
+    factor_up, rhs_value = finished(aug)
     return (proposal, predicted[None], factor_up, rhs_value)
 
 

time: 592 us -> 324 us (0.55)
  waiting for transfers between devices: 246 us -> 0.01 us
  Pallas kernels: 177 us -> 232 us
  other arithmetic: 62 us -> 7.43 us
  between operations: 16.3 us -> 1.46 us
    psum x1 -> x0, waiting for transfers between devices: 246 us -> none  [per_device(): aug = lax.psum(aug, ('tm', 'space'))]
    pallas_call x0 -> x1, Pallas kernels: none -> 55.9 us  [finished(): pl.pallas_call(finish_kernel, out_shape=(jax.ShapeDtypeStruct((256, 256),...]
    another operation x12 -> x2, other arithmetic: 55.8 us -> 1.29 us  [the longest x6 33.9 us: finish_factor(): factor_low = jnp.linalg.cholesky(information)]
  transfers between devices with their start and end apart: 3 -> 2, of which waited for: 1 -> 0; matrix products, arithmetic and copies ran while one was open for 1% -> 2% of each run, Pallas kernels for 0% -> 0%
where the time goes in v2:
time: 324 us
  Pallas kernels  232 us (72%)
  blocking collectives  41.8 us (13%)
  matrix products  27.8 us (9%)
  other arithmetic  7.43 us (2%)
  local copies, waits for them, and re-layouts  6.87 us (2%)
  starting transfers between devices  5.65 us (2%)
    pallas_call x1, Pallas kernels, gathered_information(): pl.pallas_call(gather_kernel, out_shape=jax.ShapeDtypeStruct((512, 128),...  177 us
    pallas_call x1, Pallas kernels, finished(): pl.pallas_call(finish_kernel, out_shape=(jax.ShapeDtypeStruct((256, 256),...  55.9 us
    all_gather x1, blocking collectives, per_device(): all_half = lax.all_gather(proposal[0].astype(jnp.bfloat16), 'space')  41.8 us
    dot_general x1, matrix products, per_device(): smooth = jnp.dot(along_rows, col_circulant, precision=lax.Precision.HIGHEST)  10.9 us
    dot_general x1, matrix products, per_device(): jnp.dot(row_band, extended_grid, precision=lax.Precision.HIGHEST)  10.9 us
  transfers between devices with their start and end apart: 2, of which 0 were waited for; matrix products, arithmetic and copies ran while one was open for 2% of the time, Pallas kernels for 0%

profile of v2, /device:TPU:1, one launch (start us, length us, event | category | flops | bytes accessed | tf_op | source)
XLA Modules:
  0.0 323.6 jit_solution(2715697582487737272)
XLA Ops:
  0.6 0.7 fusion.238
  1.3 4.4 %collective-permute-start = (f32[1,512]{1,0:T(1,128)S(1)}, f32[1,512]{1,0:T(1,128)S(1)}, u32[]{:S(2)}, u32[]{:S(2)}) collective-permute-start(f32[1,512]{1,0:T(1,128)S(1)} %get-tuple-element.34), channel_id=1, source_target_pairs={{0,1},{1,2},{2,3},{3,4},{4,5},{5,6},{6,7},{7,8},{8,9},{9,10},{10,1... | collective-permute-start | bytes 6152 | tf_op jit(solution)/shard_map/ppermute | solution.py:28
  5.7 1.3 collective-permute-start.1
  7.0 0.6 multiply_reduce_fusion
  7.6 0.6 compare_reduce_fusion
  9.0 0.7 fusion.199
  9.8 0.8 select_reduce_fusion.2
  10.6 0.7 multiply_add_fusion.1
  11.3 0.1 iota_compare_fusion
  11.3 0.1 select_reduce_fusion.1
  11.4 0.7 broadcast_select_fusion
  12.1 0.7 fusion.239
  12.8 0.6 scatter.6.tab_ref
  13.4 0.1 copy.14
  13.5 0.2 broadcast_in_dim.69
  13.7 0.3 broadcast_in_dim.70
  14.0 0.8 maximum_reduce_fusion
  14.8 0.1 reshape.145
  14.9 10.9 %fusion.39 = f32[64,64]{1,0:T(8,128)S(1)} fusion(f32[80,64]{1,0:T(8,128)S(1)} %reshape.145, f32[]{:T(128)} %bitcast.16, f32[]{:T(128)} %bitcast.15, f32[]{:T(128)} %bitcast.14, f32[]{:T(128)} %bitcast.13, f32[]{:T(128)} %bitcast.12, f32[]{:T(128)} %bitcast.11, f32[]{:T(128)} %bitcast.10, f32[]{:T(128)} %bitcast.9, f32[]{:T(128)} %bitcast.8, f32[]{:T(128)} %bitcast.7, ...), kind=kOutput, calls=%fused_computation.45 | convolution fusion | flops 4193280 | bytes 36932 | tf_op jit(solution)/shard_map/dot_general | solution.py:420
  25.8 10.9 %fusion.5 = f32[64,64]{1,0:T(8,128)S(1)} fusion(f32[64,64]{1,0:T(8,128)S(1)} %fusion.39, f32[]{:T(128)} %bitcast.16, f32[]{:T(128)} %bitcast.15, f32[]{:T(128)} %bitcast.14, f32[]{:T(128)} %bitcast.13, f32[]{:T(128)} %bitcast.12, f32[]{:T(128)} %bitcast.11, f32[]{:T(128)} %bitcast.10, f32[]{:T(128)} %bitcast.9, f32[]{:T(128)} %bitcast.8, f32[]{:T(128)} %bitcast.7, ...), kind=kOutput, calls=%fused_computation.11 | convolution fusion | flops 3403776 | bytes 32836 | tf_op jit(solution)/shard_map/dot_general | solution.py:421
  36.8 0.7 multiply_multiply_fusion
  37.5 1.4 convert_bitcast_fusion
  38.8 41.8 %all-gather = bf16[32,1,4096]{2,1,0:T(2,128)(2,1)S(1)} all-gather(bf16[1,1,4096]{2,1,0:T(2,128)(2,1)S(1)} %get-tuple-element.32), channel_id=1, replica_groups=mesh['tm'=8,'space'=32] {'space'}, dimensions={0}, use_global_device_ids=true | all-gather | bytes 270336 | tf_op jit(solution)/shard_map/all_gather | solution.py:432
  80.7 6.0 %fusion.1 = f32[1024]{0:T(1024)S(1)} fusion(pred[1024,32]{0,1:T(32,128)(4,1)S(1)} %broadcast_in_dim.70, bf16[1024,4096]{1,0:T(8,128)(2,1)} %bitcast.41, bf16[32,1,4096]{2,1,0:T(2,128)(2,1)S(1)} %all-gather), kind=kOutput, calls=%fused_computation.2 | convolution fusion | flops 268499968 | bytes 8687616 | tf_op jit(solution)/shard_map/dot_general | solution.py:433
  86.8 0.2 select_reduce_fusion
  87.0 0.1 copy.15
  87.1 0.1 reshape.147
  87.2 0.6 scatter.9.mis_ref
  87.8 176.6 %gather_information.1.aug_ref = f32[512,128]{1,0:T(8,128)} custom-call(s32[1,128]{1,0:T(1,128)} %scatter.6.tab_ref, f32[8,2048]{1,0:T(8,128)} %scatter.9.mis_ref, bf16[1,32,32,4096]{3,2,1,0:T(8,128)(2,1)} %fp_ref.1, bf16[4096,256]{1,0:T(8,128)(2,1)} %basis_ref.1), custom_call_target="tpu_custom_call" | custom-call | tf_op jit(solution)/shard_map/gather_information/pallas_call | solution.py:237
  264.4 55.9 %sum_and_factor.1 = (f32[256,256]{1,0:T(8,128)}, f32[256,128]{1,0:T(8,128)}) custom-call(f32[512,128]{1,0:T(8,128)} %gather_information.1.aug_ref), custom_call_target="tpu_custom_call" | custom-call | tf_op jit(solution)/shard_map/sum_and_factor/pallas_call | solution.py:382
  320.3 1.6 slice_reduce_fusion
  321.9 1.7 copy.23
  (12 shorter events, 0.2 us)
Async XLA Ops:
  0.6 86.1 %copy-start.1 = (bf16[1,32,32]{2,1,0:T(8,128)(2,1)S(1)}, bf16[1,32,32]{2,1,0:T(8,128)(2,1)}, u32[]{:S(2)}) copy-start(bf16[1,32,32]{2,1,0:T(8,128)(2,1)} %param.15) | copy-start | bytes 6148
  1.3 12.7 %collective-permute-start = (f32[1,512]{1,0:T(1,128)S(1)}, f32[1,512]{1,0:T(1,128)S(1)}, u32[]{:S(2)}, u32[]{:S(2)}) collective-permute-start(f32[1,512]{1,0:T(1,128)S(1)} %get-tuple-element.34), channel_id=1, source_target_pairs={{0,1},{1,2},{2,3},{3,4},{4,5},{5,6},{6,7},{7,8},{8,9},{9,10},{10,1... | collective-permute-start | bytes 6152 | tf_op jit(solution)/shard_map/ppermute | solution.py:28
  5.7 8.3 %collective-permute-start.1 = (f32[1,512]{1,0:T(1,128)S(1)}, f32[1,512]{1,0:T(1,128)S(1)}, u32[]{:S(2)}, u32[]{:S(2)}) collective-permute-start(f32[1,512]{1,0:T(1,128)S(1)} %get-tuple-element.35), channel_id=1, source_target_pairs={{1,0},{2,1},{3,2},{4,3},{5,4},{6,5},{7,6},{8,7},{9,8},{10,9},{11,1... | collective-permute-start | bytes 6152 | tf_op jit(solution)/shard_map/ppermute | solution.py:29
  86.8 236.8 %copy-start = (f32[1,32,32]{2,1,0:T(8,128)}, f32[1,32,32]{2,1,0:T(8,128)S(1)}, u32[]{:S(2)}) copy-start(f32[1,32,32]{2,1,0:T(8,128)S(1)} %broadcast_in_dim.72) | copy-start | bytes 12292

commit v3 on v1

--- a/solution.py
+++ b/solution.py
@@ -1,3 +1,5 @@
+import math
+
 import jax
 import jax.numpy as jnp
 from jax import lax
@@ -6,41 +8,56 @@
 from jax.sharding import PartitionSpec as P
 
 MESH = pl.DeviceIdType.MESH
+HIGHEST = lax.Precision.HIGHEST
 BLOCKS_HERE = 32
 JAC_SCALE = float(262144) ** (-0.5)
-
-PATCH = 64
 REACH = 8
-
-
 BETA = 0.6
 KEEP = 0.8
 
 
-def padded(shard, sides, width):
-    for axis, dim in sides:
-        devices, length = (lax.axis_size(axis), shard.shape[dim])
-        up = [(i, (i + 1) % devices) for i in range(devices - 1)]
-        down = [(j, i) for i, j in up]
-        last = lax.slice_in_dim(shard, length - width, length, axis=dim)
-        leading = lax.slice_in_dim(shard, 0, width, axis=dim)
-        before = lax.ppermute(last, axis, up)
-        after = lax.ppermute(leading, axis, down)
-        shard = jnp.concatenate([before, shard, after], axis=dim)
-    return shard
-
-
 def kernel_weights(reach):
-    offsets = jnp.abs(jnp.arange(-reach, reach + 1).astype(jnp.float32))
-    profile = (1.0 + 2.0 * offsets / reach) * jnp.exp(-2.0 * offsets / reach)
-    return profile / jnp.sqrt(jnp.sum(profile * profile))
-
-
-def finish_factor(gram_sum, projected):
-    information = jnp.eye(gram_sum.shape[0], dtype=jnp.float32) + gram_sum
-    factor_low = jnp.linalg.cholesky(information)
-    rhs_value = jax.scipy.linalg.solve_triangular(factor_low, projected, lower=True)
-    return (factor_low.T, rhs_value)
+    profile = [(1.0 + 2.0 * abs(d) / reach) * math.exp(-2.0 * abs(d) / reach) for d in range(-reach, reach + 1)]
+    norm = math.sqrt(sum(p * p for p in profile))
+    return [p / norm for p in profile]
+
+
+KERNEL = kernel_weights(REACH)
+
+
+def factor_rows(work, out_u, out_v):
+    row = lax.broadcasted_iota(jnp.int32, (32, 128), 0)
+    lane = lax.broadcasted_iota(jnp.int32, (32, 128), 1)
+    wide_row = lax.broadcasted_iota(jnp.int32, (32, 256), 0)
+    wide_lane = lax.broadcasted_iota(jnp.int32, (32, 256), 1)
+    for k in range(8):
+        k0, c0 = 32 * k, 128 * (k // 4)
+        off = k0 - c0
+        eye0 = (off + 64) % 128
+        rows = work[k0:k0 + 32, :]
+        e = jnp.where(jnp.logical_and(lane >= off, lane < off + 32), rows[:, c0:c0 + 128], 0.0)
+        e = e + (lane - eye0 == row).astype(jnp.float32)
+        for j in range(32):
+            column = jnp.where(row > j, jnp.broadcast_to(e[:, off + j:off + j + 1], (32, 128)), 0.0)
+            pivot = e[j:j + 1, off + j:off + j + 1]
+            e = e - column * (e[j:j + 1, :] * (1.0 / pivot))
+        diagonal = jnp.sum(jnp.where(lane == row + off, e, 0.0), axis=1, keepdims=True)
+        e = e * lax.rsqrt(diagonal)
+        inverse = e[:, eye0:eye0 + 32]
+        panel = jnp.dot(inverse, rows[:, c0:], preferred_element_type=jnp.float32, precision=HIGHEST)
+        upper = panel[:, :256 - c0]
+        if c0:
+            upper = jnp.concatenate([jnp.zeros((32, c0), jnp.float32), upper], axis=1)
+        upper = jnp.where(wide_lane >= wide_row + k0, upper, 0.0)
+        out_u[k0:k0 + 32, :] = upper
+        out_v[k0:k0 + 32, :] = panel[:, 256 - c0:]
+        if k < 7:
+            k1 = k0 + 32
+            c1 = 128 * (k1 // 128)
+            left = panel[:, c1 - c0:256 - c0]
+            update = lax.dot_general(left, panel[:, c1 - c0:], (((0,), (0,)), ((), ())),
+                                     preferred_element_type=jnp.float32, precision=HIGHEST)
+            work[k1:, c1:] = work[k1:, c1:] - update[k1 - c1:]
 
 
 PA, PB, QA, QB = 368, 816, 560, 560
@@ -48,10 +65,37 @@
 LAG1, LAG2 = 2, 4
 
 
-def gather_kernel(tab_ref, mis_ref, fp_ref, basis_ref, aug_ref,
-                  own_f, sib_f, tiles, jac, jac_out, tab_v, tab_own, tab_sib,
-                  load_sem, pair_send, pair_recv, tree_recv, cross_recv, tree_send, cross_send,
-                  jac_send, jac_recv):
+def weight(position):
+    return KERNEL[REACH + position]
+
+
+def smoothing_matrices():
+    lane = lax.broadcasted_iota(jnp.int32, (128, 128), 1)
+    source = lax.broadcasted_iota(jnp.int32, (128, 128), 0)
+    same = lax.div(lane, 64) == lax.div(source, 64)
+    gap = lax.rem(source - lane + 64 + REACH, 64)
+    columns = jnp.zeros((128, 128), jnp.float32)
+    for b in range(-REACH, REACH + 1):
+        columns = columns + jnp.where(jnp.logical_and(same, gap == b + REACH), weight(b), 0.0)
+    row = lax.broadcasted_iota(jnp.int32, (32, 48), 0)
+    shift = lax.broadcasted_iota(jnp.int32, (32, 48), 1) - 8 - row
+    bands = []
+    for offset in (0, 1, -1):
+        band = jnp.zeros((32, 48), jnp.float32)
+        for d in range(-4, 5):
+            if abs(2 * d + offset) <= REACH:
+                band = band + jnp.where(shift == d, weight(2 * d + offset), 0.0)
+        bands.append(band)
+    return columns, bands
+
+
+def step_kernel(flux_ref, noise_ref, prior_ref, table_ref, sound_ref, pick_ref, fp_ref, basis_ref,
+                proposal_ref, predicted_ref, u_ref, v_ref,
+                own_f, sib_f, tiles, halves, jac, jac_out, accs, extended, tab_v, tab_own, tab_sib,
+                aug, parts, sums, full, work,
+                load_sem, pair_send, pair_recv, tree_recv, cross_recv, tree_send, cross_send,
+                jac_send, jac_recv, half_send, half_recv, halo_send, halo_recv,
+                send_a, recv_a, send_b, recv_b, send_c, recv_c):
     t = lax.axis_index("tm")
     s = lax.axis_index("space")
     x, c = lax.div(t, 2), lax.rem(t, 2)
@@ -70,16 +114,51 @@
     own_load.start()
     fp_load = pltpu.make_async_copy(fp_ref.at[0], own_f.at[pl.ds(0, count)], load_sem.at[1])
     fp_load.start()
-    tab_load = pltpu.make_async_copy(tab_ref, tab_own, load_sem.at[2])
+    tab_load = pltpu.make_async_copy(table_ref, tab_own, load_sem.at[2])
     tab_load.start()
 
+    a = c * 8 + z
+    b = x * 4 + y
+
+    def in_a(k):
+        other = lax.rem(a + k, 16)
+        return other, (x * 2 + lax.div(other, 8), y * 8 + lax.rem(other, 8))
+
+    def in_b(k):
+        other = lax.rem(b + k, 16)
+        return other, (lax.div(other, 4) * 2 + c, lax.rem(other, 4) * 8 + z)
+
+    next_tile = (t, lax.rem(s + 1, 32))
+    last_tile = (t, lax.rem(s + 31, 32))
     barrier = pltpu.get_barrier_semaphore()
-    for other in (sibling, z_up, z_down, y_up, y_down, x_up, x_down):
+
+    def greet(k, carry):
+        for group in (in_a, in_b):
+            pl.semaphore_signal(barrier, inc=1, device_id=group(k)[1], device_id_type=MESH)
+        return carry
+
+    lax.fori_loop(1, 16, greet, 0)
+    for other in (next_tile, last_tile):
         pl.semaphore_signal(barrier, inc=1, device_id=other, device_id_type=MESH)
-    pl.semaphore_wait(barrier, 7)
+    pl.semaphore_wait(barrier, 32)
+
+    to_next = pltpu.make_async_remote_copy(
+        src_ref=noise_ref.at[pl.ds(24, 8)], dst_ref=extended.at[pl.ds(0, 8)], send_sem=halo_send.at[0],
+        recv_sem=halo_recv.at[0], device_id=next_tile, device_id_type=MESH)
+    to_last = pltpu.make_async_remote_copy(
+        src_ref=noise_ref.at[pl.ds(0, 8)], dst_ref=extended.at[pl.ds(40, 8)], send_sem=halo_send.at[1],
+        recv_sem=halo_recv.at[1], device_id=last_tile, device_id_type=MESH)
+
+    @pl.when(s < 31)
+    def _():
+        to_next.start()
+
+    @pl.when(s > 0)
+    def _():
+        to_last.start()
 
     tab_swap = pltpu.make_async_remote_copy(
-        src_ref=tab_ref, dst_ref=tab_v, send_sem=pair_send.at[0], recv_sem=pair_recv.at[0],
+        src_ref=table_ref, dst_ref=tab_v, send_sem=pair_send.at[0], recv_sem=pair_recv.at[0],
         device_id=sibling, device_id_type=MESH)
     tab_swap.start()
     own_load.wait()
@@ -137,6 +216,26 @@
                     send(rows, tile, cross_send.at[0], cross_recv.at[0, tile], x_up).start()
                     send(rows, tile, cross_send.at[1], cross_recv.at[1, tile], x_down).start()
 
+    def send_half(tile, device):
+        region = halves.at[tile]
+        return pltpu.make_async_remote_copy(
+            src_ref=region, dst_ref=region, send_sem=half_send, recv_sem=half_recv.at[tile],
+            device_id=device, device_id_type=MESH)
+
+    def forward_half(n):
+        tile, dy, dz = tile_of(n)
+
+        @pl.when(n > 0)
+        def _():
+            send_half(tile, sibling).wait_recv()
+
+        for go, device in ((jnp.logical_and(dy == 0, dz < 4), z_up),
+                           (jnp.logical_and(dy == 0, jnp.logical_or(dz == 0, dz > 5)), z_down),
+                           (dy < 2, y_up), (dy == 0, y_down)):
+            @pl.when(go)
+            def _():
+                send_half(tile, device).start()
+
     def pass_on(n):
         tile, _, _ = tile_of(n)
         below, above = lax.rem(x + 3, 4), lax.rem(x + 1, 4)
@@ -163,7 +262,16 @@
                 [own_f[own_a, :, ks], own_f[own_b, :, ks], sib_f[sib_a, :, ks], sib_f[sib_b, :, ks]], axis=0)
             total += jnp.dot(lhs, tiles[tile, ks, :], preferred_element_type=jnp.float32)
         total = (total * JAC_SCALE).astype(jnp.bfloat16)
+        values = halves[tile].astype(jnp.float32)
+        seen_a = jnp.zeros((32, 128), jnp.float32)
+        seen_b = jnp.zeros((32, 128), jnp.float32)
+        for k in range(32):
+            ks = pl.ds(k * 128, 128)
+            value = values[k:k + 1, :]
+            seen_a += own_f[own_a, :, ks].astype(jnp.float32) * value
+            seen_b += own_f[own_b, :, ks].astype(jnp.float32) * value
         rows = pl.ds(pl.multiple_of(tile * 64, 64), 64)
+        accs[rows, :] = jnp.concatenate([seen_a, seen_b], axis=0)
         jac[c, rows, :] = total[:64]
         jac_out[rows, :] = total[64:]
         pltpu.make_async_remote_copy(
@@ -177,6 +285,37 @@
     fp_swap.start()
     own_f[count] = jnp.zeros(own_f.shape[1:], own_f.dtype)
     sib_f[count] = jnp.zeros(sib_f.shape[1:], sib_f.dtype)
+    columns, (band_even, band_up, band_down) = smoothing_matrices()
+    extended[8:40, :] = noise_ref[...]
+
+    @pl.when(s > 0)
+    def _():
+        to_next.wait_recv()
+
+    @pl.when(s == 0)
+    def _():
+        extended[0:8, :] = jnp.zeros((8, 128), jnp.float32)
+
+    @pl.when(s < 31)
+    def _():
+        to_last.wait_recv()
+
+    @pl.when(s == 31)
+    def _():
+        extended[40:48, :] = jnp.zeros((8, 128), jnp.float32)
+
+    def exact(p, q):
+        return jnp.dot(p, q, precision=HIGHEST, preferred_element_type=jnp.float32)
+
+    mixed = exact(extended[...], columns)
+    swapped = jnp.concatenate([mixed[:, 64:], mixed[:, :64]], axis=1)
+    lane = lax.broadcasted_iota(jnp.int32, (32, 128), 1)
+    smooth = exact(band_even, mixed) + jnp.where(
+        lane < 64, exact(band_up, swapped), exact(band_down, swapped))
+    proposal = KEEP * flux_ref[...] + BETA * prior_ref[...] * smooth
+    proposal_ref[...] = proposal
+    halves[s] = proposal.astype(jnp.bfloat16)
+    forward_half(0)
     tab_swap.wait()
     sib_load = pltpu.make_async_copy(tab_v, tab_sib, load_sem.at[3])
     sib_load.start()
@@ -189,6 +328,7 @@
         @pl.when(n < 32)
         def _():
             forward(n)
+            forward_half(n)
         if RX:
             @pl.when(jnp.logical_and(n >= LAG1 + 1, n < 32 + LAG1))
             def _():
@@ -217,100 +357,142 @@
         src_ref=jac_out, dst_ref=jac.at[1 - c], send_sem=jac_send, recv_sem=jac_recv,
         device_id=sibling, device_id_type=MESH)
     whole.wait()
+    region = halves.at[pl.ds(0, 31)]
+    pltpu.make_async_copy(region, region, half_send).wait()
+
+    @pl.when(s < 31)
+    def _():
+        to_next.wait_send()
+
+    @pl.when(s > 0)
+    def _():
+        to_last.wait_send()
+
     low, high = jac[0], jac[1]
 
     def gram(a, b):
         return lax.dot_general(a, b, (((0,), (0,)), ((), ())), preferred_element_type=jnp.float32)
 
-    aug_ref[0:128, :] = gram(low, low)
-    aug_ref[128:256, :] = gram(low, high)
-    aug_ref[256:384, :] = gram(high, high)
-    mis = mis_ref[...]
+    aug[0:128, :] = gram(low, low)
+    aug[128:256, :] = gram(low, high)
+    aug[256:384, :] = gram(high, high)
+    seen_rows = lax.dot_general(jnp.ones((8, 128), jnp.float32), accs[...], (((1,), (1,)), ((), ())),
+                                precision=HIGHEST, preferred_element_type=jnp.float32)
+    mis = sound_ref[...] - seen_rows
     mis_a = mis.astype(jnp.bfloat16)
     rest = mis - mis_a.astype(jnp.float32)
     mis_b = rest.astype(jnp.bfloat16)
     mis_c = (rest - mis_b.astype(jnp.float32)).astype(jnp.bfloat16)
-    aug_ref[384:, :] = jnp.zeros((128, 128), jnp.float32)
+    aug[384:, :] = jnp.zeros((128, 128), jnp.float32)
     for k, side in enumerate((low, high)):
         part = sum(jnp.dot(m, side, preferred_element_type=jnp.float32) for m in (mis_c, mis_b, mis_a))
-        aug_ref[384 + 8 * k:392 + 8 * k, :] = part
-
-
-def gathered_information(table, misfit, footprints, basis):
+        aug[384 + 8 * k:392 + 8 * k, :] = part
+
+    def rows(index):
+        return pl.ds(pl.multiple_of(index * 32, 32), 32)
+
+    def scatter(k, carry):
+        other, device = in_a(k)
+        pltpu.make_async_remote_copy(
+            src_ref=aug.at[rows(other)], dst_ref=parts.at[k - 1], send_sem=send_a, recv_sem=recv_a,
+            device_id=device, device_id_type=MESH).start()
+        return carry
+
+    lax.fori_loop(1, 16, scatter, 0)
+
+    def settle(region, send_sem, recv_sem):
+        pltpu.make_async_copy(region, region, send_sem).wait()
+        pltpu.make_async_copy(region, region, recv_sem).wait()
+
+    seen = jnp.sum(accs[...].reshape(64, 32, 128), axis=-1)
+    predicted_ref[...] = exact(pick_ref[...], seen)
+    settle(parts, send_a, recv_a)
+    own = aug[rows(a), :]
+    for k in range(15):
+        own = own + parts[k]
+    sums[b] = own
+
+    def exchange(k, carry):
+        _, device = in_b(k)
+        pltpu.make_async_remote_copy(
+            src_ref=sums.at[b], dst_ref=sums.at[b], send_sem=send_b, recv_sem=recv_b,
+            device_id=device, device_id_type=MESH).start()
+        return carry
+
+    lax.fori_loop(1, 16, exchange, 0)
+    settle(parts, send_b, recv_b)
+    total = sums[0]
+    for k in range(1, 16):
+        total = total + sums[k]
+    full[rows(a), :] = total
+
+    def spread(k, carry):
+        _, device = in_a(k)
+        pltpu.make_async_remote_copy(
+            src_ref=full.at[rows(a)], dst_ref=full.at[rows(a)], send_sem=send_c, recv_sem=recv_c,
+            device_id=device, device_id_type=MESH).start()
+        return carry
+
+    lax.fori_loop(1, 16, spread, 0)
+    settle(parts, send_c, recv_c)
+    square = (128, 128)
+    eye = (lax.broadcasted_iota(jnp.int32, square, 0) == lax.broadcasted_iota(jnp.int32, square, 1))
+    eye = eye.astype(jnp.float32)
+    rhs = full[384:512, :].T
+    work[0:128, 0:128] = full[0:128, :] + eye
+    work[0:128, 128:256] = full[128:256, :]
+    work[128:256, 128:256] = full[256:384, :] + eye
+    work[0:128, 256:384] = rhs
+    work[128:256, 256:384] = jnp.concatenate([rhs[:, 8:], rhs[:, :8]], axis=1)
+    factor_rows(work, u_ref, v_ref)
+
+
+def whole_step(flux, noise, prior, table, sound, pick, footprints, basis):
     vm = pl.BlockSpec(memory_space=pltpu.VMEM)
     hbm = pl.BlockSpec(memory_space=pl.ANY)
     dma = pltpu.SemaphoreType.DMA
+    f32, bf16 = jnp.float32, jnp.bfloat16
     return pl.pallas_call(
-        gather_kernel,
-        out_shape=jax.ShapeDtypeStruct((512, 128), jnp.float32),
-        in_specs=[vm, vm, hbm, hbm],
-        out_specs=vm,
+        step_kernel,
+        out_shape=(jax.ShapeDtypeStruct((32, 128), f32), jax.ShapeDtypeStruct((32, 32), f32),
+                   jax.ShapeDtypeStruct((256, 256), f32), jax.ShapeDtypeStruct((256, 128), f32)),
+        in_specs=[vm, vm, vm, vm, vm, vm, hbm, hbm],
+        out_specs=(vm, vm, vm, vm),
         scratch_shapes=[
-            pltpu.VMEM((33, 32, 4096), jnp.bfloat16),
-            pltpu.VMEM((33, 32, 4096), jnp.bfloat16),
-            pltpu.VMEM((32, 4096, 128), jnp.bfloat16),
-            pltpu.VMEM((2, 2048, 128), jnp.bfloat16),
-            pltpu.VMEM((2048, 128), jnp.bfloat16),
-            pltpu.VMEM((1, 128), jnp.int32),
-            pltpu.SMEM((1, 128), jnp.int32),
-            pltpu.SMEM((1, 128), jnp.int32),
+            pltpu.VMEM((33, 32, 4096), bf16), pltpu.VMEM((33, 32, 4096), bf16),
+            pltpu.VMEM((32, 4096, 128), bf16), pltpu.VMEM((32, 32, 128), bf16),
+            pltpu.VMEM((2, 2048, 128), bf16), pltpu.VMEM((2048, 128), bf16),
+            pltpu.VMEM((2048, 128), f32), pltpu.VMEM((48, 128), f32),
+            pltpu.VMEM((1, 128), jnp.int32), pltpu.SMEM((1, 128), jnp.int32), pltpu.SMEM((1, 128), jnp.int32),
+            pltpu.VMEM((512, 128), f32), pltpu.VMEM((15, 32, 128), f32), pltpu.VMEM((16, 32, 128), f32),
+            pltpu.VMEM((512, 128), f32), pltpu.VMEM((256, 384), f32),
             dma((4,)), dma((2,)), dma((2,)), dma((5, 32)), dma((4, 32)), dma((5,)), dma((4,)),
-            dma, dma,
+            dma, dma, dma, dma((32,)), dma((2,)), dma((2,)),
+            dma, dma, dma, dma, dma, dma,
         ],
         compiler_params=pltpu.CompilerParams(
             collective_id=0, has_side_effects=True, vmem_limit_bytes=60 * 1024 * 1024),
-        name="gather_information",
-    )(table, misfit, footprints, basis)
+        name="assimilate",
+    )(flux, noise, prior, table, sound, pick, footprints, basis)
 
 
 def per_device(flux, noise, prior_scale, footprints, soundings, targets, basis):
     block_count = footprints.shape[1]
-    obs_count = footprints.shape[2]
-    cell_count = footprints.shape[3]
-    patch_edge = PATCH
     tile_count = 32
-    weights = kernel_weights(REACH)
-    extended = padded(noise, (("space", 1),), REACH * patch_edge)
-    extended_grid = extended.reshape(patch_edge + 2 * REACH, patch_edge)
-    row_offset = jnp.arange(patch_edge + 2 * REACH)[None, :] - jnp.arange(patch_edge)[:, None]
-    col_offset = (
-        jnp.arange(patch_edge)[:, None] - jnp.arange(patch_edge)[None, :] + REACH
-    ) % patch_edge
-    row_band = jnp.zeros((patch_edge, patch_edge + 2 * REACH), jnp.float32)
-    col_circulant = jnp.zeros((patch_edge, patch_edge), jnp.float32)
-    for position in range(2 * REACH + 1):
-        row_band = row_band + weights[position] * (row_offset == position).astype(jnp.float32)
-        col_circulant = col_circulant + weights[position] * (col_offset == position).astype(
-            jnp.float32
-        )
-    along_rows = jnp.dot(row_band, extended_grid, precision=lax.Precision.HIGHEST)
-    smooth = jnp.dot(along_rows, col_circulant, precision=lax.Precision.HIGHEST)
-    proposal = KEEP * flux + BETA * prior_scale[None, :] * smooth.reshape(1, cell_count)
     destination = targets[0, :, 0]
-    dest_onehot = destination[:, None] == jnp.arange(tile_count)[None, :]
-    counts = dest_onehot.astype(jnp.int32)
+    counts = (destination[:, None] == jnp.arange(tile_count)[None, :]).astype(jnp.int32)
     slot_rank = jnp.sum((jnp.cumsum(counts, axis=0) - counts) * counts, axis=1)
     slot_of = destination * 2 + slot_rank
     slot_match = slot_of[None, :] == jnp.arange(2 * tile_count)[:, None]
     source_of = jnp.sum(jnp.where(slot_match, jnp.arange(block_count)[None, :] + 1, 0), axis=1) - 1
     source_of = jnp.where(source_of < 0, block_count, source_of)
     table = jnp.zeros((1, 128), jnp.int32).at[0, : 2 * tile_count].set(source_of)
-    all_half = lax.all_gather(proposal[0].astype(jnp.bfloat16), "space")
-    every = jnp.dot(
-        footprints[0].reshape(block_count * obs_count, cell_count), all_half.T,
-        preferred_element_type=jnp.float32,
-    ).reshape(block_count, obs_count, tile_count)
-    predicted = jnp.sum(jnp.where(dest_onehot[:, None, :], every, 0.0), axis=2)
-    misfit = soundings[0].astype(jnp.float32) - predicted
-    misfit_slots = jnp.sum(jnp.where(slot_match[:, :, None], misfit[None], 0.0), axis=1)
-    misfit_rows = jnp.zeros((8, 2048), jnp.float32).at[0].set(misfit_slots.reshape(-1))
-    aug = gathered_information(table, misfit_rows, footprints, basis)
-    aug = lax.psum(aug, ("tm", "space"))
-    cross = aug[128:256]
-    gram = jnp.block([[aug[0:128], cross], [cross.T, aug[256:384]]])
-    projected = jnp.concatenate([aug[384], aug[392]])
-    factor_up, rhs_value = finish_factor(gram, projected)
-    return (proposal, predicted[None], factor_up, rhs_value)
+    pick = slot_match.T.astype(jnp.float32)
+    sound = jnp.sum(jnp.where(slot_match[:, :, None], soundings[0].astype(jnp.float32)[None], 0.0), axis=1)
+    proposal, predicted, factor_up, rhs_value = whole_step(
+        flux.reshape(32, 128), noise.reshape(32, 128), prior_scale.reshape(32, 128),
+        table, sound.reshape(1, 2048), pick, footprints, basis)
+    return (proposal.reshape(1, 4096), predicted[None], factor_up, rhs_value[:, 0])
 
 
 def solution(mesh):

time: 592 us -> 237 us (0.40)
  waiting for transfers between devices: 246 us -> 0 us
  other arithmetic: 62 us -> 5.31 us
  Pallas kernels: 177 us -> 223 us
  blocking collectives: 41.8 us -> 0 us
  matrix products: 28.9 us -> 0 us
  between operations: 16.3 us -> 0.66 us
    psum x1 -> x0, waiting for transfers between devices: 246 us -> none  [per_device(): aug = lax.psum(aug, ('tm', 'space'))]
    another operation x12 -> x2, other arithmetic: 55.8 us -> 1.29 us  [the longest x6 33.9 us: finish_factor(): factor_low = jnp.linalg.cholesky(information)]
    pallas_call x1, Pallas kernels: 177 us -> 223 us  [whole_step(): pl.pallas_call(step_kernel, out_shape=(jax.ShapeDtypeStruct((32, 128), f3...]
    all_gather x1 -> x0, blocking collectives: 41.8 us -> none  [per_device(): all_half = lax.all_gather(proposal[0].astype(jnp.bfloat16), 'space')]
    dot_general x3 -> x0, matrix products: 27.8 us -> none  [the longest x1 10.9 us: per_device(): smooth = jnp.dot(along_rows, col_circulant, precision=lax.Precision.HIGHEST)]
  transfers between devices with their start and end apart: 3 -> 0, of which waited for: 1 -> 0; matrix products, arithmetic and copies ran while one was open for 1% -> 0% of each run, Pallas kernels for 0% -> 0%
where the time goes in v3:
time: 237 us; the launch traced here: 236 us
  Pallas kernels  223 us (94%)
  local copies, waits for them, and re-layouts  7.18 us (3%)
  other arithmetic  5.31 us (2%)
    pallas_call x1, Pallas kernels, whole_step(): pl.pallas_call(step_kernel, out_shape=(jax.ShapeDtypeStruct((32, 128), f3...  223 us

profile of v3, /device:TPU:1, one launch (start us, length us, event | category | flops | bytes accessed | tf_op | source)
XLA Modules:
  0.0 236.1 jit_solution(3256248085720797633)
XLA Ops:
  0.6 0.6 compare_reduce_fusion
  1.3 0.7 bitcast_convert_fusion
  2.0 0.7 fusion
  2.7 0.1 reduce_window_sum.11
  2.8 0.8 select_reduce_fusion.2
  3.6 0.7 iota_add_fusion
  4.3 0.1 select_reduce_fusion.1
  4.3 0.6 broadcast_select_fusion
  5.0 0.5 scatter.4.table_ref
  5.5 0.1 iota_compare_fusion.1
  5.6 0.2 select_reduce_fusion
  5.8 0.7 fusion.1.pick_ref
  6.5 0.1 copy.11
  6.6 0.7 reshape.100.sound_ref
  7.2 223.0 %assimilate.1 = (f32[32,128]{1,0:T(8,128)}, f32[32,32]{1,0:T(8,128)}, f32[256,256]{1,0:T(8,128)}, f32[256,128]{1,0:T(8,128)}) custom-call(f32[32,128]{1,0:T(8,128)} %bitcast.12, f32[32,128]{1,0:T(8,128)} %bitcast.13, f32[32,128]{1,0:T(8,128)} %bitcast.14, s32[1,128]{1,0:T(1,128)} %scatter.4.table_ref, f32[1,2048]{1,0:T(1,128)} %reshape.100.sound_ref, ...), custom_call_target="tpu_custom_call" | custom-call | tf_op jit(solution)/shard_map/assimilate/pallas_call | solution.py:455
  230.2 1.6 slice_reduce_fusion
  231.8 1.3 copy.15
  233.1 1.3 copy.16
  234.4 1.7 copy.17

commit v4 on v3

--- a/solution.py
+++ b/solution.py
@@ -37,10 +37,18 @@
         rows = work[k0:k0 + 32, :]
         e = jnp.where(jnp.logical_and(lane >= off, lane < off + 32), rows[:, c0:c0 + 128], 0.0)
         e = e + (lane - eye0 == row).astype(jnp.float32)
-        for j in range(32):
-            column = jnp.where(row > j, jnp.broadcast_to(e[:, off + j:off + j + 1], (32, 128)), 0.0)
-            pivot = e[j:j + 1, off + j:off + j + 1]
-            e = e - column * (e[j:j + 1, :] * (1.0 / pivot))
+        for j in range(0, 32, 8):
+            cols = [jnp.broadcast_to(e[:, off + p:off + p + 1], (32, 128)) for p in range(j, j + 8)]
+            heads = [e[p:p + 1, :] for p in range(j, j + 8)]
+            for i in range(8):
+                p = j + i
+                scale = 1.0 / cols[i][p:p + 1, :]
+                below = jnp.where(row > p, cols[i], 0.0)
+                scaled = heads[i] * scale
+                for l in range(i + 1, 8):
+                    heads[l] = heads[l] - cols[i][j + l:j + l + 1, :] * scaled
+                    cols[l] = cols[l] - below * (cols[l][p:p + 1, :] * scale)
+                e = e - below * scaled
         diagonal = jnp.sum(jnp.where(lane == row + off, e, 0.0), axis=1, keepdims=True)
         e = e * lax.rsqrt(diagonal)
         inverse = e[:, eye0:eye0 + 32]
@@ -67,6 +75,20 @@
 
 def weight(position):
     return KERNEL[REACH + position]
+
+
+def slot_tables(target):
+    row = lax.broadcasted_iota(jnp.int32, (32, 32), 0)
+    lane = lax.broadcasted_iota(jnp.int32, (32, 32), 1)
+    across = jnp.broadcast_to(target, (32, 32))
+    down = jnp.sum(jnp.where(row == lane, across, 0), axis=1, keepdims=True)
+    earlier = jnp.logical_and(across == down, lane < row)
+    slot = 2 * down + jnp.sum(jnp.where(earlier, 1, 0), axis=1, keepdims=True)
+    slots = lax.broadcasted_iota(jnp.int32, (32, 128), 1)
+    block = lax.broadcasted_iota(jnp.int32, (32, 128), 0)
+    match = slot == slots
+    source = 32 + jnp.sum(jnp.where(match, block - 32, 0), axis=0, keepdims=True)
+    return source, jnp.where(match, 1.0, 0.0)
 
 
 def smoothing_matrices():
@@ -89,10 +111,10 @@
     return columns, bands
 
 
-def step_kernel(flux_ref, noise_ref, prior_ref, table_ref, sound_ref, pick_ref, fp_ref, basis_ref,
-                proposal_ref, predicted_ref, u_ref, v_ref,
-                own_f, sib_f, tiles, halves, jac, jac_out, accs, extended, tab_v, tab_own, tab_sib,
-                aug, parts, sums, full, work,
+def step_kernel(flux_ref, noise_ref, prior_ref, target_ref, sound_ref, fp_ref, basis_ref,
+                proposal_ref, predicted_ref, full,
+                own_f, sib_f, tiles, halves, jac, jac_out, accs, gaps, extended, square, sound_t,
+                tab_mine, tab_v, tab_own, tab_sib, aug, parts, sums,
                 load_sem, pair_send, pair_recv, tree_recv, cross_recv, tree_send, cross_send,
                 jac_send, jac_recv, half_send, half_recv, halo_send, halo_recv,
                 send_a, recv_a, send_b, recv_b, send_c, recv_c):
@@ -114,33 +136,35 @@
     own_load.start()
     fp_load = pltpu.make_async_copy(fp_ref.at[0], own_f.at[pl.ds(0, count)], load_sem.at[1])
     fp_load.start()
-    tab_load = pltpu.make_async_copy(table_ref, tab_own, load_sem.at[2])
-    tab_load.start()
-
-    a = c * 8 + z
-    b = x * 4 + y
+
+    a = t * 4 + y
+    b = z
 
     def in_a(k):
-        other = lax.rem(a + k, 16)
-        return other, (x * 2 + lax.div(other, 8), y * 8 + lax.rem(other, 8))
+        other = lax.rem(a + k, 32)
+        return other, (lax.div(other, 4), lax.rem(other, 4) * 8 + z)
 
     def in_b(k):
-        other = lax.rem(b + k, 16)
-        return other, (lax.div(other, 4) * 2 + c, lax.rem(other, 4) * 8 + z)
+        other = lax.rem(b + k, 8)
+        return other, (t, y * 8 + other)
 
     next_tile = (t, lax.rem(s + 1, 32))
     last_tile = (t, lax.rem(s + 31, 32))
     barrier = pltpu.get_barrier_semaphore()
 
-    def greet(k, carry):
-        for group in (in_a, in_b):
-            pl.semaphore_signal(barrier, inc=1, device_id=group(k)[1], device_id_type=MESH)
+    def greet_a(k, carry):
+        pl.semaphore_signal(barrier, inc=1, device_id=in_a(k)[1], device_id_type=MESH)
         return carry
 
-    lax.fori_loop(1, 16, greet, 0)
+    def greet_b(k, carry):
+        pl.semaphore_signal(barrier, inc=1, device_id=in_b(k)[1], device_id_type=MESH)
+        return carry
+
+    lax.fori_loop(1, 32, greet_a, 0)
+    lax.fori_loop(1, 8, greet_b, 0)
     for other in (next_tile, last_tile):
         pl.semaphore_signal(barrier, inc=1, device_id=other, device_id_type=MESH)
-    pl.semaphore_wait(barrier, 32)
+    pl.semaphore_wait(barrier, 40)
 
     to_next = pltpu.make_async_remote_copy(
         src_ref=noise_ref.at[pl.ds(24, 8)], dst_ref=extended.at[pl.ds(0, 8)], send_sem=halo_send.at[0],
@@ -157,10 +181,6 @@
     def _():
         to_last.start()
 
-    tab_swap = pltpu.make_async_remote_copy(
-        src_ref=table_ref, dst_ref=tab_v, send_sem=pair_send.at[0], recv_sem=pair_recv.at[0],
-        device_id=sibling, device_id_type=MESH)
-    tab_swap.start()
     own_load.wait()
 
     def send(rows, tile, send_sem, recv_sem, device):
@@ -272,6 +292,10 @@
             seen_b += own_f[own_b, :, ks].astype(jnp.float32) * value
         rows = pl.ds(pl.multiple_of(tile * 64, 64), 64)
         accs[rows, :] = jnp.concatenate([seen_a, seen_b], axis=0)
+        lane = lax.broadcasted_iota(jnp.int32, (32, 128), 1)
+        gaps[rows, :] = jnp.concatenate(
+            [jnp.where(lane == own_a, sound_t[...], 0.0) - seen_a,
+             jnp.where(lane == own_b, sound_t[...], 0.0) - seen_b], axis=0)
         jac[c, rows, :] = total[:64]
         jac_out[rows, :] = total[64:]
         pltpu.make_async_remote_copy(
@@ -279,6 +303,17 @@
             device_id=sibling, device_id_type=MESH).start()
 
     forward(0)
+    source, match = slot_tables(target_ref[...])
+    tab_mine[...] = source
+    tab_load = pltpu.make_async_copy(tab_mine, tab_own, load_sem.at[2])
+    tab_load.start()
+    tab_swap = pltpu.make_async_remote_copy(
+        src_ref=tab_mine, dst_ref=tab_v, send_sem=pair_send.at[0], recv_sem=pair_recv.at[0],
+        device_id=sibling, device_id_type=MESH)
+    tab_swap.start()
+    square[...] = jnp.zeros(square.shape, jnp.float32)
+    square[0:32, 0:32] = sound_ref[...].astype(jnp.float32)
+    sound_t[...] = square[...].T[0:32, :]
     fp_swap = pltpu.make_async_remote_copy(
         src_ref=fp_ref.at[0], dst_ref=sib_f.at[pl.ds(0, count)], send_sem=pair_send.at[1],
         recv_sem=pair_recv.at[1], device_id=sibling, device_id_type=MESH)
@@ -376,9 +411,8 @@
     aug[0:128, :] = gram(low, low)
     aug[128:256, :] = gram(low, high)
     aug[256:384, :] = gram(high, high)
-    seen_rows = lax.dot_general(jnp.ones((8, 128), jnp.float32), accs[...], (((1,), (1,)), ((), ())),
-                                precision=HIGHEST, preferred_element_type=jnp.float32)
-    mis = sound_ref[...] - seen_rows
+    mis = lax.dot_general(jnp.ones((8, 128), jnp.float32), gaps[...], (((1,), (1,)), ((), ())),
+                          precision=HIGHEST, preferred_element_type=jnp.float32)
     mis_a = mis.astype(jnp.bfloat16)
     rest = mis - mis_a.astype(jnp.float32)
     mis_b = rest.astype(jnp.bfloat16)
@@ -389,7 +423,7 @@
         aug[384 + 8 * k:392 + 8 * k, :] = part
 
     def rows(index):
-        return pl.ds(pl.multiple_of(index * 32, 32), 32)
+        return pl.ds(pl.multiple_of(index * 16, 16), 16)
 
     def scatter(k, carry):
         other, device = in_a(k)
@@ -398,17 +432,17 @@
             device_id=device, device_id_type=MESH).start()
         return carry
 
-    lax.fori_loop(1, 16, scatter, 0)
+    lax.fori_loop(1, 32, scatter, 0)
 
     def settle(region, send_sem, recv_sem):
         pltpu.make_async_copy(region, region, send_sem).wait()
         pltpu.make_async_copy(region, region, recv_sem).wait()
 
     seen = jnp.sum(accs[...].reshape(64, 32, 128), axis=-1)
-    predicted_ref[...] = exact(pick_ref[...], seen)
+    predicted_ref[...] = exact(match[:, :64], seen)
     settle(parts, send_a, recv_a)
     own = aug[rows(a), :]
-    for k in range(15):
+    for k in range(31):
         own = own + parts[k]
     sums[b] = own
 
@@ -419,10 +453,10 @@
             device_id=device, device_id_type=MESH).start()
         return carry
 
-    lax.fori_loop(1, 16, exchange, 0)
-    settle(parts, send_b, recv_b)
+    lax.fori_loop(1, 8, exchange, 0)
+    settle(parts.at[pl.ds(0, 7)], send_b, recv_b)
     total = sums[0]
-    for k in range(1, 16):
+    for k in range(1, 8):
         total = total + sums[k]
     full[rows(a), :] = total
 
@@ -433,8 +467,13 @@
             device_id=device, device_id_type=MESH).start()
         return carry
 
-    lax.fori_loop(1, 16, spread, 0)
+    lax.fori_loop(1, 32, spread, 0)
     settle(parts, send_c, recv_c)
+
+
+def factor_kernel(full, proposal_in, predicted_in, proposal_ref, predicted_ref, u_ref, v_ref, work, solved):
+    proposal_ref[...] = proposal_in[...]
+    predicted_ref[...] = predicted_in[...]
     square = (128, 128)
     eye = (lax.broadcasted_iota(jnp.int32, square, 0) == lax.broadcasted_iota(jnp.int32, square, 1))
     eye = eye.astype(jnp.float32)
@@ -444,28 +483,30 @@
     work[128:256, 128:256] = full[256:384, :] + eye
     work[0:128, 256:384] = rhs
     work[128:256, 256:384] = jnp.concatenate([rhs[:, 8:], rhs[:, :8]], axis=1)
-    factor_rows(work, u_ref, v_ref)
-
-
-def whole_step(flux, noise, prior, table, sound, pick, footprints, basis):
+    factor_rows(work, u_ref, solved)
+    v_ref[:, 0:128] = solved[0:128, :].T[0:1, :]
+    v_ref[:, 128:256] = solved[128:256, :].T[0:1, :]
+
+
+def whole_step(flux, noise, prior, target, sound, footprints, basis):
     vm = pl.BlockSpec(memory_space=pltpu.VMEM)
     hbm = pl.BlockSpec(memory_space=pl.ANY)
     dma = pltpu.SemaphoreType.DMA
-    f32, bf16 = jnp.float32, jnp.bfloat16
-    return pl.pallas_call(
+    f32, bf16, i32 = jnp.float32, jnp.bfloat16, jnp.int32
+    shapes = (jax.ShapeDtypeStruct((32, 128), f32), jax.ShapeDtypeStruct((32, 32), f32))
+    proposal, predicted, summed = pl.pallas_call(
         step_kernel,
-        out_shape=(jax.ShapeDtypeStruct((32, 128), f32), jax.ShapeDtypeStruct((32, 32), f32),
-                   jax.ShapeDtypeStruct((256, 256), f32), jax.ShapeDtypeStruct((256, 128), f32)),
-        in_specs=[vm, vm, vm, vm, vm, vm, hbm, hbm],
-        out_specs=(vm, vm, vm, vm),
+        out_shape=shapes + (jax.ShapeDtypeStruct((512, 128), f32),),
+        in_specs=[vm, vm, vm, vm, vm, hbm, hbm],
+        out_specs=(vm, vm, vm),
         scratch_shapes=[
             pltpu.VMEM((33, 32, 4096), bf16), pltpu.VMEM((33, 32, 4096), bf16),
             pltpu.VMEM((32, 4096, 128), bf16), pltpu.VMEM((32, 32, 128), bf16),
             pltpu.VMEM((2, 2048, 128), bf16), pltpu.VMEM((2048, 128), bf16),
-            pltpu.VMEM((2048, 128), f32), pltpu.VMEM((48, 128), f32),
-            pltpu.VMEM((1, 128), jnp.int32), pltpu.SMEM((1, 128), jnp.int32), pltpu.SMEM((1, 128), jnp.int32),
-            pltpu.VMEM((512, 128), f32), pltpu.VMEM((15, 32, 128), f32), pltpu.VMEM((16, 32, 128), f32),
-            pltpu.VMEM((512, 128), f32), pltpu.VMEM((256, 384), f32),
+            pltpu.VMEM((2048, 128), f32), pltpu.VMEM((2048, 128), f32), pltpu.VMEM((48, 128), f32),
+            pltpu.VMEM((128, 128), f32), pltpu.VMEM((32, 128), f32),
+            pltpu.VMEM((1, 128), i32), pltpu.VMEM((1, 128), i32), pltpu.SMEM((1, 128), i32), pltpu.SMEM((1, 128), i32),
+            pltpu.VMEM((512, 128), f32), pltpu.VMEM((31, 16, 128), f32), pltpu.VMEM((8, 16, 128), f32),
             dma((4,)), dma((2,)), dma((2,)), dma((5, 32)), dma((4, 32)), dma((5,)), dma((4,)),
             dma, dma, dma, dma((32,)), dma((2,)), dma((2,)),
             dma, dma, dma, dma, dma, dma,
@@ -473,26 +514,22 @@
         compiler_params=pltpu.CompilerParams(
             collective_id=0, has_side_effects=True, vmem_limit_bytes=60 * 1024 * 1024),
         name="assimilate",
-    )(flux, noise, prior, table, sound, pick, footprints, basis)
+    )(flux, noise, prior, target, sound, footprints, basis)
+    return pl.pallas_call(
+        factor_kernel,
+        out_shape=shapes + (jax.ShapeDtypeStruct((256, 256), f32), jax.ShapeDtypeStruct((1, 256), f32)),
+        in_specs=[vm, vm, vm],
+        out_specs=(vm, vm, vm, vm),
+        scratch_shapes=[pltpu.VMEM((256, 384), f32), pltpu.VMEM((256, 128), f32)],
+        name="factor",
+    )(summed, proposal, predicted)
 
 
 def per_device(flux, noise, prior_scale, footprints, soundings, targets, basis):
-    block_count = footprints.shape[1]
-    tile_count = 32
-    destination = targets[0, :, 0]
-    counts = (destination[:, None] == jnp.arange(tile_count)[None, :]).astype(jnp.int32)
-    slot_rank = jnp.sum((jnp.cumsum(counts, axis=0) - counts) * counts, axis=1)
-    slot_of = destination * 2 + slot_rank
-    slot_match = slot_of[None, :] == jnp.arange(2 * tile_count)[:, None]
-    source_of = jnp.sum(jnp.where(slot_match, jnp.arange(block_count)[None, :] + 1, 0), axis=1) - 1
-    source_of = jnp.where(source_of < 0, block_count, source_of)
-    table = jnp.zeros((1, 128), jnp.int32).at[0, : 2 * tile_count].set(source_of)
-    pick = slot_match.T.astype(jnp.float32)
-    sound = jnp.sum(jnp.where(slot_match[:, :, None], soundings[0].astype(jnp.float32)[None], 0.0), axis=1)
     proposal, predicted, factor_up, rhs_value = whole_step(
         flux.reshape(32, 128), noise.reshape(32, 128), prior_scale.reshape(32, 128),
-        table, sound.reshape(1, 2048), pick, footprints, basis)
-    return (proposal.reshape(1, 4096), predicted[None], factor_up, rhs_value[:, 0])
+        targets.reshape(1, 32), soundings.reshape(32, 32), footprints, basis)
+    return (proposal.reshape(1, 4096), predicted[None], factor_up, rhs_value.reshape(256))
 
 
 def solution(mesh):

time: 237 us -> 205 us (0.86)
  Pallas kernels: 223 us -> 204 us
  local copies, waits for them, and re-layouts: 7.18 us -> 0 us
  other arithmetic: 5.31 us -> 0 us
    pallas_call x1 -> x2, Pallas kernels: 223 us -> 204 us  [the longest x1 191 us: whole_step(): pl.pallas_call(step_kernel, out_shape=shapes + (jax.ShapeDtypeStruct((512...]
    unnamed x3 -> x0, local copies, waits for them, and re-layouts: 4.31 us -> none
where the time goes in v4:
time: 205 us
  Pallas kernels  204 us (100%)
    pallas_call x1, Pallas kernels, whole_step(): pl.pallas_call(step_kernel, out_shape=shapes + (jax.ShapeDtypeStruct((512...  191 us
    pallas_call x1, Pallas kernels, whole_step(): pl.pallas_call(factor_kernel, out_shape=shapes + (jax.ShapeDtypeStruct((2...  12.7 us

profile of v4, /device:TPU:1, one launch (start us, length us, event | category | flops | bytes accessed | tf_op | source)
XLA Modules:
  0.0 204.5 jit_solution(6147989890692289525)
XLA Ops:
  0.6 191.2 %assimilate.1 = (f32[32,128]{1,0:T(8,128)}, f32[32,32]{1,0:T(8,128)}, f32[512,128]{1,0:T(8,128)}) custom-call(f32[32,128]{1,0:T(8,128)} %bitcast.8, f32[32,128]{1,0:T(8,128)} %bitcast.9, f32[32,128]{1,0:T(8,128)} %bitcast.10, s32[1,32]{1,0:T(1,128)} %bitcast.12, bf16[32,32]{1,0:T(8,128)(2,1)} %bitcast.11, bf16[1,32,32,4096]{3,2,1,0:T(8,128)(2,1)} %fp_ref.1, ...), custom_call_target="tpu_custom_call" | custom-call | tf_op jit(solution)/shard_map/assimilate/pallas_call | solution.py:497
  191.9 12.7 %factor.1 = (f32[32,128]{1,0:T(8,128)}, f32[32,32]{1,0:T(8,128)}, f32[256,256]{1,0:T(8,128)}, f32[1,256]{1,0:T(1,128)}) custom-call(f32[512,128]{1,0:T(8,128)} %get-tuple-element.11.full, f32[32,128]{1,0:T(8,128)} %get-tuple-element.12.proposal_in, f32[32,32]{1,0:T(8,128)} %get-tuple-element.13.predicted_in), custom_call_target="tpu_custom_call" | custom-call | tf_op jit(solution)/shard_map/factor/pallas_call | solution.py:518

commit v5 on v4

--- a/solution.py
+++ b/solution.py
@@ -68,9 +68,10 @@
             work[k1:, c1:] = work[k1:, c1:] - update[k1 - c1:]
 
 
-PA, PB, QA, QB = 368, 816, 560, 560
-RX = 448
-LAG1, LAG2 = 2, 4
+PA, PB, QA, QB = 512, 896, 576, 576
+RX = 384
+AHEAD_SHARED, AHEAD_ACROSS = 6, 0
+LAG_CROSS, LAG_WORK = 3, 2
 
 
 def weight(position):
@@ -114,7 +115,7 @@
 def step_kernel(flux_ref, noise_ref, prior_ref, target_ref, sound_ref, fp_ref, basis_ref,
                 proposal_ref, predicted_ref, full,
                 own_f, sib_f, tiles, halves, jac, jac_out, accs, gaps, extended, square, sound_t,
-                tab_mine, tab_v, tab_own, tab_sib, aug, parts, sums,
+                tab_mine, tab_v, tab_own, tab_sib, aug, parts, sums, accum,
                 load_sem, pair_send, pair_recv, tree_recv, cross_recv, tree_send, cross_send,
                 jac_send, jac_recv, half_send, half_recv, halo_send, halo_recv,
                 send_a, recv_a, send_b, recv_b, send_c, recv_c):
@@ -202,16 +203,25 @@
     def piece(owner, first, size):
         return pl.ds(pl.multiple_of(shared_base + owner * RX + first, 16), size)
 
-    def tile_of(n):
-        col, i = lax.div(n, 8), lax.rem(n, 8)
-        dy = col + lax.div(col, 2) * (1 - 2 * lax.rem(col, 2))
+    def placed(dy, i):
         dz = lax.rem(lax.div(i + 1, 2) * (2 * lax.rem(i, 2) - 1) + 8, 8)
         tile = lax.rem(y - dy + 4, 4) * 8 + lax.rem(z - dz + 8, 8)
         return tile, dy, dz
 
-    def forward(n):
-        tile, dy, dz = tile_of(n)
-        for k, (rows, along_z_first, long_up, shared) in enumerate(classes):
+    def tile_of(n):
+        part = lax.div(n, 8)
+        middle = lax.rem(lax.div(part + 1, 2), 2)
+        dy = middle * (1 + 2 * lax.rem(n, 2)) + 2 * lax.div(part, 3)
+        return placed(dy, middle * lax.div(n - 8, 2) + (1 - middle) * lax.rem(n, 8))
+
+    def across_of(n):
+        col = lax.rem(n, 4)
+        return placed(col + lax.div(col, 2) * (1 - 2 * lax.rem(col, 2)), lax.div(n, 4))
+
+    def forward(n, chosen):
+        for k in chosen:
+            rows, along_z_first, long_up, shared = classes[k]
+            tile, dy, dz = tile_of(n) if along_z_first else across_of(n)
             hi_z, hi_y = (4, 2) if long_up else (3, 1)
 
             @pl.when(n > 0)
@@ -264,6 +274,26 @@
         send(piece(above, 0, RX), tile, cross_send.at[1], cross_recv.at[1, tile], sibling).wait_recv()
         send(piece(above, half, half), tile, cross_send.at[3], cross_recv.at[3, tile], x_down).start()
 
+    def blocks_of(tile):
+        return (tab_own[0, tile * 2], tab_own[0, tile * 2 + 1]), (tab_sib[0, tile * 2], tab_sib[0, tile * 2 + 1])
+
+    def accumulate(tile, begin, end):
+        (own_a, own_b), (sib_a, sib_b) = blocks_of(tile)
+        total = accum[tile]
+        for k in range(begin, end, 384):
+            ks = pl.ds(k, min(384, end - k))
+            lhs = jnp.concatenate(
+                [own_f[own_a, :, ks], own_f[own_b, :, ks], sib_f[sib_a, :, ks], sib_f[sib_b, :, ks]], axis=0)
+            total += jnp.dot(lhs, tiles[tile, ks, :], preferred_element_type=jnp.float32)
+        accum[tile] = total
+
+    def finish_tile(tile, carry):
+        total = (accum[tile] * JAC_SCALE).astype(jnp.bfloat16)
+        rows = pl.ds(pl.multiple_of(tile * 64, 64), 64)
+        jac[c, rows, :] = total[:64]
+        jac_out[rows, :] = total[64:]
+        return carry
+
     def multiply(n):
         tile, _, _ = tile_of(n)
         if RX:
@@ -273,15 +303,9 @@
             def _():
                 send(piece(far, 0, half), tile, cross_send.at[2], cross_recv.at[2, tile], sibling).wait_recv()
                 send(piece(far, half, half), tile, cross_send.at[3], cross_recv.at[3, tile], sibling).wait_recv()
-        own_a, own_b = tab_own[0, tile * 2], tab_own[0, tile * 2 + 1]
-        sib_a, sib_b = tab_sib[0, tile * 2], tab_sib[0, tile * 2 + 1]
-        total = jnp.zeros((128, 128), jnp.float32)
-        for k in range(4096 // 512):
-            ks = pl.ds(k * 512, 512)
-            lhs = jnp.concatenate(
-                [own_f[own_a, :, ks], own_f[own_b, :, ks], sib_f[sib_a, :, ks], sib_f[sib_b, :, ks]], axis=0)
-            total += jnp.dot(lhs, tiles[tile, ks, :], preferred_element_type=jnp.float32)
-        total = (total * JAC_SCALE).astype(jnp.bfloat16)
+        (own_a, own_b), _ = blocks_of(tile)
+        accumulate(tile, 0, PA + PB)
+        accumulate(tile, PA + PB + QA + QB, 4096)
         values = halves[tile].astype(jnp.float32)
         seen_a = jnp.zeros((32, 128), jnp.float32)
         seen_b = jnp.zeros((32, 128), jnp.float32)
@@ -296,13 +320,8 @@
         gaps[rows, :] = jnp.concatenate(
             [jnp.where(lane == own_a, sound_t[...], 0.0) - seen_a,
              jnp.where(lane == own_b, sound_t[...], 0.0) - seen_b], axis=0)
-        jac[c, rows, :] = total[:64]
-        jac_out[rows, :] = total[64:]
-        pltpu.make_async_remote_copy(
-            src_ref=jac_out.at[rows], dst_ref=jac.at[c, rows], send_sem=jac_send, recv_sem=jac_recv,
-            device_id=sibling, device_id_type=MESH).start()
-
-    forward(0)
+
+    forward(0, (4, 0, 1, 2, 3))
     source, match = slot_tables(target_ref[...])
     tab_mine[...] = source
     tab_load = pltpu.make_async_copy(tab_mine, tab_own, load_sem.at[2])
@@ -356,30 +375,55 @@
     sib_load.start()
     tab_load.wait()
     sib_load.wait()
-    fp_load.wait()
-    fp_swap.wait()
+
+    def stream(n, ahead, limit, item):
+        @pl.when(n <= ahead)
+        def _():
+            item(2 * n - 1)
+            item(2 * n)
+
+        @pl.when(jnp.logical_and(n > ahead, n + ahead < limit))
+        def _():
+            item(n + ahead)
+
+    def cross_item(m):
+        @pl.when(m < 32)
+        def _():
+            forward(m, (4,))
+
+        @pl.when(m > LAG_CROSS)
+        def _():
+            pass_on(m - LAG_CROSS)
 
     def step(n, carry):
+        stream(n, AHEAD_SHARED, 32 + LAG_CROSS, cross_item)
+
         @pl.when(n < 32)
         def _():
-            forward(n)
+            forward(n, (0, 1))
             forward_half(n)
-        if RX:
-            @pl.when(jnp.logical_and(n >= LAG1 + 1, n < 32 + LAG1))
-            def _():
-                pass_on(n - LAG1)
-        lag = LAG2 if RX else 0
-
-        @pl.when(n >= lag)
-        def _():
-            multiply(n - lag)
-        return carry
-
-    if RX:
-        lax.fori_loop(1, 32 + LAG2, step, 0)
-    else:
-        multiply(jnp.int32(0))
-        lax.fori_loop(1, 32, step, 0)
+        stream(n, AHEAD_ACROSS, 32, lambda m: forward(m, (2, 3)))
+
+        @pl.when(n == LAG_WORK)
+        def _():
+            fp_load.wait()
+            fp_swap.wait()
+
+        @pl.when(n >= LAG_WORK)
+        def _():
+            multiply(n - LAG_WORK)
+            accumulate(across_of(n - LAG_WORK)[0], PA + PB, PA + PB + QA + QB)
+        return carry
+
+    accum[...] = jnp.zeros(accum.shape, jnp.float32)
+    lax.fori_loop(1, 32 + LAG_WORK, step, 0)
+    lax.fori_loop(0, 32, finish_tile, 0)
+    whole = pltpu.make_async_remote_copy(
+        src_ref=jac_out, dst_ref=jac.at[c], send_sem=jac_send, recv_sem=jac_recv,
+        device_id=sibling, device_id_type=MESH)
+    whole.start()
+    mis = lax.dot_general(jnp.ones((8, 128), jnp.float32), gaps[...], (((1,), (1,)), ((), ())),
+                          precision=HIGHEST, preferred_element_type=jnp.float32)
 
     for k, (rows, _, _, _) in enumerate(classes):
         region = tiles.at[pl.ds(0, 31), rows]
@@ -388,9 +432,6 @@
         for k, size in enumerate((RX, RX, half, half)):
             region = tiles.at[pl.ds(0, 31), pl.ds(0, size)]
             pltpu.make_async_copy(region, region, cross_send.at[k]).wait()
-    whole = pltpu.make_async_remote_copy(
-        src_ref=jac_out, dst_ref=jac.at[1 - c], send_sem=jac_send, recv_sem=jac_recv,
-        device_id=sibling, device_id_type=MESH)
     whole.wait()
     region = halves.at[pl.ds(0, 31)]
     pltpu.make_async_copy(region, region, half_send).wait()
@@ -411,8 +452,6 @@
     aug[0:128, :] = gram(low, low)
     aug[128:256, :] = gram(low, high)
     aug[256:384, :] = gram(high, high)
-    mis = lax.dot_general(jnp.ones((8, 128), jnp.float32), gaps[...], (((1,), (1,)), ((), ())),
-                          precision=HIGHEST, preferred_element_type=jnp.float32)
     mis_a = mis.astype(jnp.bfloat16)
     rest = mis - mis_a.astype(jnp.float32)
     mis_b = rest.astype(jnp.bfloat16)
@@ -506,7 +545,7 @@
             pltpu.VMEM((2048, 128), f32), pltpu.VMEM((2048, 128), f32), pltpu.VMEM((48, 128), f32),
             pltpu.VMEM((128, 128), f32), pltpu.VMEM((32, 128), f32),
             pltpu.VMEM((1, 128), i32), pltpu.VMEM((1, 128), i32), pltpu.SMEM((1, 128), i32), pltpu.SMEM((1, 128), i32),
-            pltpu.VMEM((512, 128), f32), pltpu.VMEM((31, 16, 128), f32), pltpu.VMEM((8, 16, 128), f32),
+            pltpu.VMEM((512, 128), f32), pltpu.VMEM((31, 16, 128), f32), pltpu.VMEM((8, 16, 128), f32), pltpu.VMEM((32, 128, 128), f32),
             dma((4,)), dma((2,)), dma((2,)), dma((5, 32)), dma((4, 32)), dma((5,)), dma((4,)),
             dma, dma, dma, dma((32,)), dma((2,)), dma((2,)),
             dma, dma, dma, dma, dma, dma,

time: 205 us -> 185 us (0.902)
  Pallas kernels: 204 us -> 185 us
    pallas_call x1, Pallas kernels: 191 us -> 172 us  [whole_step(): pl.pallas_call(step_kernel, out_shape=shapes + (jax.ShapeDtypeStruct((512...]
where the time goes in v5:
time: 185 us
  Pallas kernels  185 us (100%)
    pallas_call x1, Pallas kernels, whole_step(): pl.pallas_call(step_kernel, out_shape=shapes + (jax.ShapeDtypeStruct((512...  172 us
    pallas_call x1, Pallas kernels, whole_step(): pl.pallas_call(factor_kernel, out_shape=shapes + (jax.ShapeDtypeStruct((2...  12.7 us

profile of v5, /device:TPU:1, one launch (start us, length us, event | category | flops | bytes accessed | tf_op | source)
XLA Modules:
  0.0 185.3 jit_solution(4722188697224930743)
XLA Ops:
  0.6 172.0 %assimilate.1 = (f32[32,128]{1,0:T(8,128)}, f32[32,32]{1,0:T(8,128)}, f32[512,128]{1,0:T(8,128)}) custom-call(f32[32,128]{1,0:T(8,128)} %bitcast.8, f32[32,128]{1,0:T(8,128)} %bitcast.9, f32[32,128]{1,0:T(8,128)} %bitcast.10, s32[1,32]{1,0:T(1,128)} %bitcast.12, bf16[32,32]{1,0:T(8,128)(2,1)} %bitcast.11, bf16[1,32,32,4096]{3,2,1,0:T(8,128)(2,1)} %fp_ref.1, ...), custom_call_target="tpu_custom_call" | custom-call | tf_op jit(solution)/shard_map/assimilate/pallas_call | solution.py:536
  172.6 12.7 %factor.1 = (f32[32,128]{1,0:T(8,128)}, f32[32,32]{1,0:T(8,128)}, f32[256,256]{1,0:T(8,128)}, f32[1,256]{1,0:T(1,128)}) custom-call(f32[512,128]{1,0:T(8,128)} %get-tuple-element.11.full, f32[32,128]{1,0:T(8,128)} %get-tuple-element.12.proposal_in, f32[32,32]{1,0:T(8,128)} %get-tuple-element.13.predicted_in), custom_call_target="tpu_custom_call" | custom-call | tf_op jit(solution)/shard_map/factor/pallas_call | solution.py:557

commit v6 on v5

--- a/solution.py
+++ b/solution.py
@@ -68,10 +68,10 @@
             work[k1:, c1:] = work[k1:, c1:] - update[k1 - c1:]
 
 
-PA, PB, QA, QB = 512, 896, 576, 576
-RX = 384
-AHEAD_SHARED, AHEAD_ACROSS = 6, 0
-LAG_CROSS, LAG_WORK = 3, 2
+PA, PB, QA, QB = 352, 928, 576, 448
+RX = 448
+AHEAD = 11
+LAG_CROSS, LAG_WORK = 5, 2
 
 
 def weight(position):
@@ -321,7 +321,7 @@
             [jnp.where(lane == own_a, sound_t[...], 0.0) - seen_a,
              jnp.where(lane == own_b, sound_t[...], 0.0) - seen_b], axis=0)
 
-    forward(0, (4, 0, 1, 2, 3))
+    forward(0, (4, 0, 2))
     source, match = slot_tables(target_ref[...])
     tab_mine[...] = source
     tab_load = pltpu.make_async_copy(tab_mine, tab_own, load_sem.at[2])
@@ -376,16 +376,6 @@
     tab_load.wait()
     sib_load.wait()
 
-    def stream(n, ahead, limit, item):
-        @pl.when(n <= ahead)
-        def _():
-            item(2 * n - 1)
-            item(2 * n)
-
-        @pl.when(jnp.logical_and(n > ahead, n + ahead < limit))
-        def _():
-            item(n + ahead)
-
     def cross_item(m):
         @pl.when(m < 32)
         def _():
@@ -395,14 +385,23 @@
         def _():
             pass_on(m - LAG_CROSS)
 
+    def early_item(m, carry):
+        cross_item(m)
+        return carry
+
     def step(n, carry):
-        stream(n, AHEAD_SHARED, 32 + LAG_CROSS, cross_item)
+        @pl.when(n < 32)
+        def _():
+            forward(n, (2, 3))
+
+        @pl.when(n + AHEAD < 32 + LAG_CROSS)
+        def _():
+            cross_item(n + AHEAD)
 
         @pl.when(n < 32)
         def _():
             forward(n, (0, 1))
             forward_half(n)
-        stream(n, AHEAD_ACROSS, 32, lambda m: forward(m, (2, 3)))
 
         @pl.when(n == LAG_WORK)
         def _():
@@ -415,6 +414,11 @@
             accumulate(across_of(n - LAG_WORK)[0], PA + PB, PA + PB + QA + QB)
         return carry
 
+    lax.fori_loop(1, 2, early_item, 0)
+    forward(0, (3,))
+    lax.fori_loop(2, 6, early_item, 0)
+    forward(0, (1,))
+    lax.fori_loop(6, 12, early_item, 0)
     accum[...] = jnp.zeros(accum.shape, jnp.float32)
     lax.fori_loop(1, 32 + LAG_WORK, step, 0)
     lax.fori_loop(0, 32, finish_tile, 0)

time: 185 us -> 179 us (0.968)
  Pallas kernels: 185 us -> 178 us
    pallas_call x1, Pallas kernels: 172 us -> 166 us  [whole_step(): pl.pallas_call(step_kernel, out_shape=shapes + (jax.ShapeDtypeStruct((512...]
where the time goes in v6:
time: 179 us
  Pallas kernels  178 us (99%)
    pallas_call x1, Pallas kernels, whole_step(): pl.pallas_call(step_kernel, out_shape=shapes + (jax.ShapeDtypeStruct((512...  166 us
    pallas_call x1, Pallas kernels, whole_step(): pl.pallas_call(factor_kernel, out_shape=shapes + (jax.ShapeDtypeStruct((2...  12.7 us

profile of v6, /device:TPU:1, one launch (start us, length us, event | category | flops | bytes accessed | tf_op | source)
XLA Modules:
  0.0 178.9 jit_solution(644879031765492485)
XLA Ops:
  0.6 165.6 %assimilate.1 = (f32[32,128]{1,0:T(8,128)}, f32[32,32]{1,0:T(8,128)}, f32[512,128]{1,0:T(8,128)}) custom-call(f32[32,128]{1,0:T(8,128)} %bitcast.8, f32[32,128]{1,0:T(8,128)} %bitcast.9, f32[32,128]{1,0:T(8,128)} %bitcast.10, s32[1,32]{1,0:T(1,128)} %bitcast.12, bf16[32,32]{1,0:T(8,128)(2,1)} %bitcast.11, bf16[1,32,32,4096]{3,2,1,0:T(8,128)(2,1)} %fp_ref.1, ...), custom_call_target="tpu_custom_call" | custom-call | tf_op jit(solution)/shard_map/assimilate/pallas_call | solution.py:540
  166.2 12.7 %factor.1 = (f32[32,128]{1,0:T(8,128)}, f32[32,32]{1,0:T(8,128)}, f32[256,256]{1,0:T(8,128)}, f32[1,256]{1,0:T(1,128)}) custom-call(f32[512,128]{1,0:T(8,128)} %get-tuple-element.11.full, f32[32,128]{1,0:T(8,128)} %get-tuple-element.12.proposal_in, f32[32,32]{1,0:T(8,128)} %get-tuple-element.13.predicted_in), custom_call_target="tpu_custom_call" | custom-call | tf_op jit(solution)/shard_map/factor/pallas_call | solution.py:561

commit v7 on v6

--- a/solution.py
+++ b/solution.py
@@ -68,10 +68,10 @@
             work[k1:, c1:] = work[k1:, c1:] - update[k1 - c1:]
 
 
-PA, PB, QA, QB = 352, 928, 576, 448
+PA, PB, QA, QB = 368, 912, 656, 368
 RX = 448
 AHEAD = 11
-LAG_CROSS, LAG_WORK = 5, 2
+LAG_CROSS, LAG_WORK = 6, 2
 
 
 def weight(position):
@@ -89,7 +89,9 @@
     block = lax.broadcasted_iota(jnp.int32, (32, 128), 0)
     match = slot == slots
     source = 32 + jnp.sum(jnp.where(match, block - 32, 0), axis=0, keepdims=True)
-    return source, jnp.where(match, 1.0, 0.0)
+    even = jnp.where(slot == 2 * lane, 1.0, 0.0)
+    odd = jnp.where(slot == 2 * lane + 1, 1.0, 0.0)
+    return source, even, odd
 
 
 def smoothing_matrices():
@@ -315,14 +317,16 @@
             seen_a += own_f[own_a, :, ks].astype(jnp.float32) * value
             seen_b += own_f[own_b, :, ks].astype(jnp.float32) * value
         rows = pl.ds(pl.multiple_of(tile * 64, 64), 64)
-        accs[rows, :] = jnp.concatenate([seen_a, seen_b], axis=0)
+        seen = lax.dot_general(jnp.ones((8, 128), jnp.float32), jnp.concatenate([seen_a, seen_b], axis=0),
+                               (((1,), (1,)), ((), ())), precision=HIGHEST, preferred_element_type=jnp.float32)
+        accs[pl.ds(tile, 1), 0:64] = seen[0:1, :]
         lane = lax.broadcasted_iota(jnp.int32, (32, 128), 1)
         gaps[rows, :] = jnp.concatenate(
             [jnp.where(lane == own_a, sound_t[...], 0.0) - seen_a,
              jnp.where(lane == own_b, sound_t[...], 0.0) - seen_b], axis=0)
 
     forward(0, (4, 0, 2))
-    source, match = slot_tables(target_ref[...])
+    source, even, odd = slot_tables(target_ref[...])
     tab_mine[...] = source
     tab_load = pltpu.make_async_copy(tab_mine, tab_own, load_sem.at[2])
     tab_load.start()
@@ -453,8 +457,9 @@
     def gram(a, b):
         return lax.dot_general(a, b, (((0,), (0,)), ((), ())), preferred_element_type=jnp.float32)
 
-    aug[0:128, :] = gram(low, low)
-    aug[128:256, :] = gram(low, high)
+    upper_rows = gram(low, jnp.concatenate([low, high], axis=1))
+    aug[0:128, :] = upper_rows[:, 0:128]
+    aug[128:256, :] = upper_rows[:, 128:256]
     aug[256:384, :] = gram(high, high)
     mis_a = mis.astype(jnp.bfloat16)
     rest = mis - mis_a.astype(jnp.float32)
@@ -481,8 +486,7 @@
         pltpu.make_async_copy(region, region, send_sem).wait()
         pltpu.make_async_copy(region, region, recv_sem).wait()
 
-    seen = jnp.sum(accs[...].reshape(64, 32, 128), axis=-1)
-    predicted_ref[...] = exact(match[:, :64], seen)
+    predicted_ref[...] = exact(even, accs[:, 0:32]) + exact(odd, accs[:, 32:64])
     settle(parts, send_a, recv_a)
     own = aug[rows(a), :]
     for k in range(31):
@@ -546,7 +550,7 @@
             pltpu.VMEM((33, 32, 4096), bf16), pltpu.VMEM((33, 32, 4096), bf16),
             pltpu.VMEM((32, 4096, 128), bf16), pltpu.VMEM((32, 32, 128), bf16),
             pltpu.VMEM((2, 2048, 128), bf16), pltpu.VMEM((2048, 128), bf16),
-            pltpu.VMEM((2048, 128), f32), pltpu.VMEM((2048, 128), f32), pltpu.VMEM((48, 128), f32),
+            pltpu.VMEM((32, 128), f32), pltpu.VMEM((2048, 128), f32), pltpu.VMEM((48, 128), f32),
             pltpu.VMEM((128, 128), f32), pltpu.VMEM((32, 128), f32),
             pltpu.VMEM((1, 128), i32), pltpu.VMEM((1, 128), i32), pltpu.SMEM((1, 128), i32), pltpu.SMEM((1, 128), i32),
             pltpu.VMEM((512, 128), f32), pltpu.VMEM((31, 16, 128), f32), pltpu.VMEM((8, 16, 128), f32), pltpu.VMEM((32, 128, 128), f32),

time: 179 us -> 178 us (level)
  no operation moved by 1% of the time
where the time goes in v7:
time: 178 us
  Pallas kernels  178 us (100%)
    pallas_call x1, Pallas kernels, whole_step(): pl.pallas_call(step_kernel, out_shape=shapes + (jax.ShapeDtypeStruct((512...  165 us
    pallas_call x1, Pallas kernels, whole_step(): pl.pallas_call(factor_kernel, out_shape=shapes + (jax.ShapeDtypeStruct((2...  12.7 us

profile of v7, /device:TPU:1, one launch (start us, length us, event | category | flops | bytes accessed | tf_op | source)
XLA Modules:
  0.0 178.3 jit_solution(627528490892849373)
XLA Ops:
  0.6 165.0 %assimilate.1 = (f32[32,128]{1,0:T(8,128)}, f32[32,32]{1,0:T(8,128)}, f32[512,128]{1,0:T(8,128)}) custom-call(f32[32,128]{1,0:T(8,128)} %bitcast.8, f32[32,128]{1,0:T(8,128)} %bitcast.9, f32[32,128]{1,0:T(8,128)} %bitcast.10, s32[1,32]{1,0:T(1,128)} %bitcast.12, bf16[32,32]{1,0:T(8,128)(2,1)} %bitcast.11, bf16[1,32,32,4096]{3,2,1,0:T(8,128)(2,1)} %fp_ref.1, ...), custom_call_target="tpu_custom_call" | custom-call | tf_op jit(solution)/shard_map/assimilate/pallas_call | solution.py:544
  165.6 12.7 %factor.1 = (f32[32,128]{1,0:T(8,128)}, f32[32,32]{1,0:T(8,128)}, f32[256,256]{1,0:T(8,128)}, f32[1,256]{1,0:T(1,128)}) custom-call(f32[512,128]{1,0:T(8,128)} %get-tuple-element.11.full, f32[32,128]{1,0:T(8,128)} %get-tuple-element.12.proposal_in, f32[32,32]{1,0:T(8,128)} %get-tuple-element.13.predicted_in), custom_call_target="tpu_custom_call" | custom-call | tf_op jit(solution)/shard_map/factor/pallas_call | solution.py:565
